TPU v7x, 32 devices: a whole 2x2x4 slice. The times are simulated.
32 devices in a mesh: seq: 4 (over x, core), exp: 2 (over y), ff: 4 (over z).
Axes of the slice: x: 2, y: 2, z: 4, core: 2. Of those that a mesh axis runs over, the one named last changes fastest.
Arguments:
- query_proj: bfloat16 [2, 512, 2560], P('exp', 'seq', 'ff'), may hold values from -85 to 85
- key_proj: bfloat16 [2, 512, 512], P('exp', 'seq', 'ff'), may hold values from -4.2 to 4.2
- value_proj: bfloat16 [2, 512, 512], P('exp', 'seq', 'ff'), may hold values from -6 to 6
- residual: bfloat16 [2, 512, 2560], P('exp', 'seq', 'ff'), may hold values from -60 to 60
- norm_gain: float32 [2560], P('ff'), may hold values from 0.5 to 2
- router_logit: float32 [2, 512], P('exp', 'seq'), may hold values from 1 to 6
- expert_ids: int32 [2, 512, 1], P('exp', 'seq'), may hold values from 0 to 1; in each aligned block of 128 rows (0 to 127, 128 to 255, ..., all dimensions but the last counted through in order) at most 96 rows name the same one
- gate_weight: bfloat16 [2, 2560, 4096], P('exp', None, ('seq', 'ff')), may hold values from -0.125 to 0.125
- up_weight: bfloat16 [2, 2560, 4096], P('exp', None, ('seq', 'ff')), may hold values from -0.125 to 0.125
- down_weight: bfloat16 [2, 4096, 2560], P('exp', ('seq', 'ff')), may hold values from -0.125 to 0.125
Outputs:
- layer_out: bfloat16 [2, 512, 2560], P('exp', 'seq', 'ff')
Inputs may be any that keep to these rules, and one draw needn't show every extreme that they name: `expert_ids`: within each aligned block of 128 positions of a span (the positions of one index of seq), no expert is named by more than 96 tokens, and in some blocks an expert is named by exactly 96.
All inputs are finite; a program needn't handle non-finite values.
Results may differ from a plain program's by a relative error of at most 0.015.
Values may be sent and summed in bfloat16 or wider, within the bound.
No kernel may reach another device: no remote copies, remote signals or barrier semaphores. Data moves between devices by JAX's collectives and lax.ppermute only.
A program may use at most 64 MiB of HBM per device.

v0:
```python
import jax
import jax.numpy as jnp
from jax import lax
from jax.sharding import PartitionSpec as P

HD = 128
HEADS = 20
KVH = 4
D = 2560


floor_score = -1e30
norm_eps = 1e-05


def passed_along(value, axis, steps):
    count = lax.axis_size(axis)
    initial, last = (max(0, -steps), min(count, count - steps))
    return lax.ppermute(value, axis, [(source, source + steps) for source in range(initial, last)])


def fold_block(carry, queries, first, keys_in, values_in, start):
    running_max, running_sum, accumulated = carry
    kv_local = queries.shape[1]
    key_rows = keys_in.reshape(keys_in.shape[0], kv_local, HD)
    value_rows = values_in.reshape(values_in.shape[0], kv_local, HD)
    scores = jnp.einsum(
        "qagd,kad->agqk", queries, key_rows, preferred_element_type=jnp.float32
    ) * HD ** (-0.5)
    query_pos = first + lax.iota(jnp.int32, queries.shape[0])
    key_pos = start + lax.iota(jnp.int32, keys_in.shape[0])
    allowed = (key_pos[None, :] <= query_pos[:, None]) & (key_pos[None, :] >= 0)
    masked = jnp.where(allowed, scores, floor_score)
    new_max = jnp.maximum(running_max, jnp.max(masked, axis=-1))
    weights = jnp.where(allowed, jnp.exp(masked - new_max[..., None]), 0.0)
    factor = jnp.exp(running_max - new_max)
    running_sum = running_sum * factor + jnp.sum(weights, axis=-1)
    accumulated = accumulated * factor[..., None] + jnp.einsum(
        "agqk,kad->agqd",
        weights.astype(jnp.bfloat16),
        value_rows,
        preferred_element_type=jnp.float32,
    )
    return (new_max, running_sum, accumulated)


def body(
    query_proj,
    key_proj,
    value_proj,
    residual,
    norm_gain,
    router_logit,
    expert_ids,
    gate_weight,
    up_weight,
    down_weight,
):
    shard_len = query_proj.shape[1]
    kv_local = key_proj.shape[2] // HD
    group = HEADS // KVH
    queries = query_proj[0].reshape(shard_len, kv_local, group, HD)
    first = lax.axis_index("seq") * shard_len
    initial = (
        jnp.full((kv_local, group, shard_len), floor_score, jnp.float32),
        jnp.zeros((kv_local, group, shard_len), jnp.float32),
        jnp.zeros((kv_local, group, shard_len, HD), jnp.float32),
    )
    stacked = jnp.stack([key_proj[0], value_proj[0]])
    carry = fold_block(initial, queries, first, key_proj[0], value_proj[0], first)
    for offset in range(1, lax.axis_size("seq")):
        arrived = passed_along(stacked, "seq", offset)
        carry = fold_block(
            carry, queries, first, arrived[0], arrived[1], first - offset * shard_len
        )
    attention = carry[2] / carry[1][..., None]
    attention = attention.transpose(2, 0, 1, 3).reshape(shard_len, kv_local * group * HD)
    stream = (residual[0].astype(jnp.float32) + attention).astype(jnp.bfloat16)
    stream_f = stream.astype(jnp.float32)
    squares = lax.psum(jnp.sum(stream_f * stream_f, axis=1), "ff")
    inverse = lax.rsqrt(squares / D + norm_eps)
    routed_in = (
        stream_f * inverse[:, None] * norm_gain[None, :] * jax.nn.sigmoid(router_logit[0])[:, None]
    )
    routed_in = routed_in.astype(jnp.bfloat16)
    expert_count = lax.axis_size("exp")
    seq_count = lax.axis_size("seq")
    ff_count = lax.axis_size("ff")
    capacity = max(2, 3 * shard_len // (2 * expert_count))
    route = expert_ids[0, :, 0]
    onehot = (route[:, None] == lax.iota(jnp.int32, expert_count)[None, :]).astype(jnp.bfloat16)
    row_iota = lax.iota(jnp.int32, shard_len)
    below = (row_iota[:, None] > row_iota[None, :]).astype(jnp.bfloat16)
    earlier = jnp.dot(below, onehot, preferred_element_type=jnp.float32)
    slot = jnp.sum(earlier * onehot.astype(jnp.float32), axis=1).astype(jnp.int32)
    target = route * capacity + slot
    selector = (target[:, None] == lax.iota(jnp.int32, expert_count * capacity)[None, :]).astype(
        jnp.bfloat16
    )
    outgoing = jnp.einsum(
        "tr,tc->rc", selector, routed_in, preferred_element_type=jnp.float32
    ).astype(jnp.bfloat16)
    quarter = D // ff_count
    width_here = gate_weight.shape[2]
    gate_parts = gate_weight[0].reshape(ff_count, quarter, width_here)
    up_parts = up_weight[0].reshape(ff_count, quarter, width_here)
    incoming = lax.all_to_all(outgoing, "exp", split_axis=0, concat_axis=0, tiled=True)
    everyone = lax.all_gather(incoming, ("seq", "ff"), axis=0, tiled=True)
    blocks = everyone.reshape(seq_count, ff_count, -1, quarter)
    gate = jnp.einsum("sfjc,fck->sjk", blocks, gate_parts, preferred_element_type=jnp.float32)
    upward = jnp.einsum("sfjc,fck->sjk", blocks, up_parts, preferred_element_type=jnp.float32)
    activated = (jax.nn.silu(gate) * upward).astype(jnp.bfloat16)
    down_parts = down_weight[0].reshape(width_here, ff_count, quarter)
    term = jnp.einsum("sjk,kfc->sfjc", activated, down_parts, preferred_element_type=jnp.float32)
    summed = lax.psum_scatter(
        term.reshape(-1, quarter).astype(jnp.bfloat16),
        ("seq", "ff"),
        scatter_dimension=0,
        tiled=True,
    )
    returned = lax.all_to_all(summed, "exp", split_axis=0, concat_axis=0, tiled=True)
    combined = jnp.dot(selector, returned, preferred_element_type=jnp.float32)
    return (stream_f + combined).astype(jnp.bfloat16)[None]


def solution(mesh):
    placed = (
        P("exp", "seq", "ff"),
        P("exp", "seq", "ff"),
        P("exp", "seq", "ff"),
        P("exp", "seq", "ff"),
        P("ff"),
        P("exp", "seq"),
        P("exp", "seq", None),
        P("exp", None, ("seq", "ff")),
        P("exp", None, ("seq", "ff")),
        P("exp", ("seq", "ff"), None),
    )
    return jax.shard_map(
        body, mesh=mesh, in_specs=placed, out_specs=P("exp", "seq", "ff"), check_vma=False
    )
```

profile of v0, /device:TPU:0, one launch (start us, length us, event | category | flops | bytes accessed | tf_op | source)
XLA Modules:
  0.0 188.0 jit_solution(18350841442558468853)
XLA Ops:
  6.5 0.9 constant_dynamic-update-slice_fusion.1
  7.4 0.8 constant_dynamic-update-slice_fusion
  8.2 4.3 %collective-permute-start.2 = (bf16[2,128,128]{2,1,0:T(8,128)(2,1)S(1)}, bf16[2,128,128]{2,1,0:T(8,128)(2,1)S(1)}, u32[]{:S(2)}, u32[]{:S(2)}) collective-permute-start(bf16[2,128,128]{2,1,0:T(8,128)(2,1)S(1)} %constant_dynamic-update-slice_fusion), channel_id=1, source_target_pairs={{0,24},{1,25},{2,26},{3,27},{4,28},{5,29},{6,30},{7,31}} | collective-permute-start | bytes 196616 | tf_op jit(solution)/shard_map/ppermute | solution.py:19
  12.5 1.3 collective-permute-start.1
  13.8 2.0 %collective-permute-start = (bf16[2,128,128]{2,1,0:T(8,128)(2,1)S(1)}, bf16[2,128,128]{2,1,0:T(8,128)(2,1)S(1)}, u32[]{:S(2)}, u32[]{:S(2)}) collective-permute-start(bf16[2,128,128]{2,1,0:T(8,128)(2,1)S(1)} %constant_dynamic-update-slice_fusion), channel_id=1, source_target_pairs={{0,8},{8,16},{16,24},{1,9},{9,17},{17,25},{2,10},{10,18},{18,26},{... | collective-permute-start | bytes 196616 | tf_op jit(solution)/shard_map/ppermute | solution.py:19
  15.9 0.9 fusion.21
  16.8 0.7 convert_add_fusion
  17.5 1.1 copy.26
  18.8 1.0 fusion.85
  19.7 0.7 divide_bitcast_fusion
  20.4 1.1 copy.40
  22.5 0.2 fusion.9
  23.0 0.2 fusion.45
  23.2 0.3 multiply_reduce_fusion
  23.6 12.1 %psum.7 = f32[128]{0:T(128)S(1)} all-reduce(f32[128]{0:T(128)S(1)} %get-tuple-element.26), channel_id=1, replica_groups=mesh['seq'=4,'exp'=2,'ff'=4] {'ff'}, use_global_device_ids=true, to_apply=%region_10.11 | all-reduce | flops 128 | bytes 1024 | tf_op jit(solution)/shard_map/psum | solution.py:80
  35.9 0.3 convolution_convert_fusion.1
  36.2 8.2 %all_to_all.24 = bf16[2,96,640]{2,1,0:T(8,128)(2,1)} all-to-all(bf16[2,96,640]{2,1,0:T(8,128)(2,1)S(1)} %bitcast.165), channel_id=1, replica_groups=mesh['seq'=4,'exp'=2,'ff'=4] {'exp'}, dimensions={0} | all-to-all | bytes 491520 | tf_op jit(solution)/shard_map/all_to_all | solution.py:107
  44.5 1.3 reshape_squeeze.8
  45.7 43.7 %all-gather.2.cloned.1.call-done = bf16[3072,640]{1,0:T(8,128)(2,1)} async-done(((bf16[192,640]{1,0:T(8,128)(2,1)}), bf16[3072,640]{1,0:T(8,128)(2,1)}) %all-gather.2.cloned.1.call-update) | async-done | bytes 3932176 | tf_op jit(solution)/shard_map/all_gather | solution.py:108
  89.5 4.7 %convolution_bitcast_fusion.1 = f32[4,192,256]{2,1,0:T(8,128)} fusion(bf16[4,4,192,640]{3,2,1,0:T(8,128)(2,1)} %bitcast.169, bf16[4,640,256,1]{2,1,0,3:T(8,128)(2,1)} %bitcast.171), kind=kOutput, calls=%fused_computation.5 | convolution fusion | flops 1006632960 | bytes 6029312 | tf_op jit(solution)/shard_map/sfjc,fck->sjk/dot_general | solution.py:110
  94.2 8.4 %convolution_convert_fusion = bf16[4,192,4,640]{3,1,2,0:T(8,128)(2,1)} fusion(bf16[256,4,640]{2,1,0:T(4,128)(2,1)S(1)} %copy-done.3, bf16[4,4,192,640]{3,2,1,0:T(8,128)(2,1)} %bitcast.170, bf16[4,640,256,1]{2,1,0,3:T(8,128)(2,1)S(1)} %bitcast.157, f32[4,192,256]{2,1,0:T(8,128)} %convolution_bitcast_fusion.1), kind=kOutput, calls=%fused_computation | convolution fusion | flops 2016411648 | bytes 11272192 | tf_op jit(solution)/shard_map/sjk,kfc->sfjc/dot_general | solution.py:114
  102.6 69.2 %reduce-scatter.2.cloned.1.call-done = bf16[192,640]{1,0:T(8,128)(2,1)} async-done(((bf16[3072,640]{1,0:T(8,128)(2,1)}), bf16[192,640]{1,0:T(8,128)(2,1)}) %reduce-scatter.2.cloned.1.call-update) | async-done | bytes 245776 | tf_op jit(solution)/shard_map/reduce_scatter | solution.py:115
  171.8 8.5 %all_to_all.25 = bf16[2,96,640]{2,1,0:T(8,128)(2,1)S(1)} all-to-all(bf16[2,96,640]{2,1,0:T(8,128)(2,1)} %bitcast.168), channel_id=1, replica_groups=mesh['seq'=4,'exp'=2,'ff'=4] {'exp'}, dimensions={0} | all-to-all | bytes 491520 | tf_op jit(solution)/shard_map/all_to_all | solution.py:121
  180.3 0.9 fusion.20
  (38 shorter events, 1.7 us)
Async XLA Ops:
  6.5 87.6 %copy-start = (bf16[1,2560,256]{2,1,0:T(8,128)(2,1)S(1)}, bf16[1,2560,256]{2,1,0:T(8,128)(2,1)}, u32[]{:S(2)}) copy-start(bf16[1,2560,256]{2,1,0:T(8,128)(2,1)} %param.18) | copy-start | bytes 3932164
  6.5 82.9 %all-gather.2.cloned.1.call-start = ((), (), s32[]{:S(2)}) async-start(), calls=%async_computation.3 | async-start | bytes 4177920 | tf_op jit(solution)/shard_map/all_gather | solution.py:108
  8.2 13.3 %collective-permute-start.2 = (bf16[2,128,128]{2,1,0:T(8,128)(2,1)S(1)}, bf16[2,128,128]{2,1,0:T(8,128)(2,1)S(1)}, u32[]{:S(2)}, u32[]{:S(2)}) collective-permute-start(bf16[2,128,128]{2,1,0:T(8,128)(2,1)S(1)} %constant_dynamic-update-slice_fusion), channel_id=1, source_target_pairs={{0,24},{1,25},{2,26},{3,27},{4,28},{5,29},{6,30},{7,31}} | collective-permute-start | bytes 196616 | tf_op jit(solution)/shard_map/ppermute | solution.py:19
  12.5 9.2 %collective-permute-start.1 = (bf16[2,128,128]{2,1,0:T(8,128)(2,1)S(1)}, bf16[2,128,128]{2,1,0:T(8,128)(2,1)S(1)}, u32[]{:S(2)}, u32[]{:S(2)}) collective-permute-start(bf16[2,128,128]{2,1,0:T(8,128)(2,1)S(1)} %constant_dynamic-update-slice_fusion), channel_id=1, source_target_pairs={{0,16},{8,24},{1,17},{9,25},{2,18},{10,26},{3,19},{11,27},{4,20},{... | collective-permute-start | bytes 196616 | tf_op jit(solution)/shard_map/ppermute | solution.py:19
  13.8 8.1 %collective-permute-start = (bf16[2,128,128]{2,1,0:T(8,128)(2,1)S(1)}, bf16[2,128,128]{2,1,0:T(8,128)(2,1)S(1)}, u32[]{:S(2)}, u32[]{:S(2)}) collective-permute-start(bf16[2,128,128]{2,1,0:T(8,128)(2,1)S(1)} %constant_dynamic-update-slice_fusion), channel_id=1, source_target_pairs={{0,8},{8,16},{16,24},{1,9},{9,17},{17,25},{2,10},{10,18},{18,26},{... | collective-permute-start | bytes 196616 | tf_op jit(solution)/shard_map/ppermute | solution.py:19
  21.7 0.8 copy-start.4
  23.2 12.7 %copy-start.1 = (bf16[1,128,640]{2,1,0:T(8,128)(2,1)S(1)}, bf16[1,128,640]{2,1,0:T(8,128)(2,1)}, u32[]{:S(2)}) copy-start(bf16[1,128,640]{2,1,0:T(8,128)(2,1)} %param.13) | copy-start | bytes 491524
  23.2 12.7 %copy-start.5 = (f32[640]{0:T(1024)S(1)}, f32[640]{0:T(1024)}, u32[]{:S(2)}) copy-start(f32[640]{0:T(1024)} %param.14) | copy-start | bytes 7684
  23.6 20.9 %copy-start.2 = (bf16[1,256,2560]{2,1,0:T(8,128)(2,1)S(1)}, bf16[1,256,2560]{2,1,0:T(8,128)(2,1)}, u32[]{:S(2)}) copy-start(bf16[1,256,2560]{2,1,0:T(8,128)(2,1)} %param.19) | copy-start | bytes 3932164
  44.4 127.4 %reduce-scatter.2.cloned.1.call-start = ((), (), s32[]{:S(2)}) async-start(), calls=%async_computation.4 | async-start | bytes 4177920 | tf_op jit(solution)/shard_map/reduce_scatter | solution.py:115
  89.5 4.7 %copy-start.3 = (bf16[256,4,640]{2,1,0:T(4,128)(2,1)S(1)}, bf16[256,4,640]{2,1,0:T(4,128)(2,1)}, u32[]{:S(2)}) copy-start(bf16[256,4,640]{2,1,0:T(4,128)(2,1)} %reshape_squeeze.8) | copy-start | bytes 3932164
Sparse Core Ops, SparseCore 0:
  44.5 44.8 all-gather.1
  102.7 69.0 reduce-scatter.1
where the time goes:
time: 189 us; the launch traced here: 188 us
  waiting for transfers between devices  113 us (60%)
  blocking collectives  28.8 us (15%)
  matrix products  17.9 us (9%)
  between operations  13.6 us (7%)
  starting transfers between devices  7.66 us (4%)
  local copies, waits for them, and re-layouts  5.21 us (3%)
  other arithmetic  1.92 us (1%)
    reduce_scatter x1, waiting for transfers between devices, body(): lax.psum_scatter(term.reshape(-1, quarter).astype(jnp.bfloat16), ('seq',...  69.2 us
    all_gather x1, waiting for transfers between devices, body(): everyone = lax.all_gather(incoming, ('seq', 'ff'), axis=0, tiled=True)  43.7 us
    psum x1, blocking collectives, body(): squares = lax.psum(jnp.sum(stream_f * stream_f, axis=1), 'ff')  12.1 us
    all_to_all x1, blocking collectives, body(): lax.all_to_all(summed, 'exp', split_axis=0, concat_axis=0, tiled=True)  8.51 us
    dot_general x1, matrix products, body(): jnp.einsum('sjk,kfc->sfjc', activated, down_parts, preferred_element_type...  8.36 us
    all_to_all x1, blocking collectives, body(): lax.all_to_all(outgoing, 'exp', split_axis=0, concat_axis=0, tiled=True)  8.16 us
    ppermute x3, starting transfers between devices, passed_along(): lax.ppermute(value, axis, [(source, source + steps) for source in range(i...  7.62 us
    dot_general x1, matrix products, body(): jnp.einsum('sfjc,fck->sjk', blocks, gate_parts, preferred_element_type=jn...  4.72 us
  transfers between devices with their start and end apart: 5, of which 2 were waited for; matrix products, arithmetic and copies ran while one was open for 4% of the time, Pallas kernels for 0%

commit v1 on v0

v1 whole, which is shorter than its diff:
```python
import functools
import jax
import jax.numpy as jnp
from jax import lax
from jax.experimental import pallas as pl
from jax.experimental.pallas import tpu as pltpu
from jax.sharding import PartitionSpec as P

HD = 128
HEADS = 20
KVH = 4

floor_score = -1e30
norm_eps = 1e-05
EXTRA = 16
f32 = jnp.float32
bf16 = jnp.bfloat16
VMEM = pl.BlockSpec(memory_space=pltpu.VMEM)
SMEM = pl.BlockSpec(memory_space=pltpu.SMEM)
RAW = pl.BlockSpec(memory_space=pltpu.HBM)


def kernel(body, out, ins, outs, limit, scratch=(), cost=None):
    return pl.pallas_call(
        body,
        out_shape=out,
        in_specs=ins,
        out_specs=outs,
        scratch_shapes=scratch,
        compiler_params=pltpu.CompilerParams(vmem_limit_bytes=limit << 20),
        cost_estimate=cost,
    )


def flip(value, later=False, **bits):
    axes = tuple(bits)
    pairs = [((), ())]
    for axis in axes:
        n = lax.axis_size(axis)
        pairs = [(s + (i,), t + (i ^ bits[axis],)) for s, t in pairs for i in range(n)]

    def flat(index):
        total = 0
        for axis, i in zip(axes, index):
            total = total * lax.axis_size(axis) + i
        return total

    pairs = [(flat(s), flat(t)) for s, t in pairs]
    if later:
        pairs = [(s, t) for s, t in pairs if s < t]
    return lax.ppermute(value, axes, pairs)


def as_column(row):
    n = row.shape[1]
    eye = lax.broadcasted_iota(jnp.int32, (n, n), 0) == lax.broadcasted_iota(jnp.int32, (n, n), 1)
    return jnp.sum(jnp.where(eye, row, 0.0), axis=1, keepdims=True)


def pack_body(k_ref, v_ref, out_ref, sems):
    shard = k_ref.shape[1]
    copies = [
        pltpu.make_async_copy(k_ref.at[0], out_ref.at[pl.ds(0, shard)], sems.at[0]),
        pltpu.make_async_copy(v_ref.at[0], out_ref.at[pl.ds(shard, shard)], sems.at[1]),
    ]
    for c in copies:
        c.start()
    for c in copies:
        c.wait()


def split(value):
    high = value.astype(bf16)
    rest = value - high.astype(f32)
    middle = rest.astype(bf16)
    return [high, middle, (rest - middle.astype(f32)).astype(bf16)]


def prep_body(experts, cap, where_ref, q_in, res_in, ids_in, logit_in, gain_in, q_out, res_out, taken_ref, *refs):
    extra_refs = refs[: 2 if experts == 2 else 1]
    lit_ref, ids_ref, logit_ref, gain_ref, sems = refs[len(extra_refs) :]
    pairs = [(ids_in, ids_ref), (logit_in, logit_ref), (gain_in, gain_ref), (q_in.at[0], q_out), (res_in.at[0], res_out)]
    copies = [pltpu.make_async_copy(x, y, sems.at[i]) for i, (x, y) in enumerate(pairs)]
    for c in copies:
        c.start()
    copies[0].wait()
    shard = ids_ref.shape[1]
    slots = taken_ref.shape[1]
    route = as_column(ids_ref[...].astype(f32)).astype(jnp.int32)
    if experts == 2:
        route = route ^ where_ref[0]
    lanes = lax.broadcasted_iota(jnp.int32, (shard, shard), 1)
    rows = lax.broadcasted_iota(jnp.int32, (shard, shard), 0)
    onehot = (lanes == route).astype(f32)
    below = (rows > lanes).astype(bf16)
    earlier = jnp.dot(below, onehot.astype(bf16), preferred_element_type=f32)
    slot = jnp.sum(earlier * onehot, axis=1, keepdims=True).astype(jnp.int32)
    target = route * cap + slot
    taken = lax.broadcasted_iota(jnp.int32, (shard, slots), 1) == target
    taken_ref[...] = taken.astype(bf16)
    copies[1].wait()
    opened = as_column(1.0 / (1.0 + jnp.exp(-logit_ref[...])))
    lit = jnp.sum(jnp.where(taken, opened, 0.0), axis=0, keepdims=True)
    lit_ref[...] = lit
    copies[2].wait()
    width = gain_ref.shape[0]
    gain = gain_ref[...].reshape(1, width)
    none = [jnp.zeros((1, width), bf16)] * 3
    if experts == 2:
        full = [split(jnp.concatenate([part, jnp.zeros((1, width - cap), f32)], axis=1)) for part in (lit[:, :cap], lit[:, cap:])]
    else:
        full = [none]
    for ref, part, top in zip(extra_refs, full, (split(gain), none)):
        ref[...] = jnp.concatenate([*top, *part, jnp.zeros((EXTRA - 6, width), bf16)], axis=0)
    for c in copies[3:]:
        c.wait()


def attend_body(group, blocks, extras, layout, where_ref, q_ref, res_ref, taken_ref, *refs):
    kv_refs = refs[:blocks]
    extra_refs = refs[blocks : blocks + extras]
    stream_ref = refs[blocks + extras]
    send_refs = refs[blocks + extras + 1 :]
    shard = q_ref.shape[0]
    me = where_ref[0]
    rows = lax.broadcasted_iota(jnp.int32, (shard, shard), 0)
    cols = lax.broadcasted_iota(jnp.int32, (shard, shard), 1)
    nt = (((1,), (1,)), ((), ()))
    pieces = []
    for h in range(q_ref.shape[1] // HD):
        g = h // group
        q = q_ref[:, h * HD : (h + 1) * HD]
        scores = []
        for b in range(blocks):
            s = lax.dot_general(q, kv_refs[b][:shard, g * HD : (g + 1) * HD], nt, preferred_element_type=f32)
            s = s * HD ** (-0.5)
            ok = cols <= rows if b == 0 else cols < jnp.where((me ^ b) < me, shard, 0)
            scores.append(jnp.where(ok, s, floor_score))
        top = jnp.max(functools.reduce(jnp.maximum, scores), axis=1, keepdims=True)
        weights = [jnp.exp(s - top) for s in scores]
        total = jnp.sum(functools.reduce(jnp.add, weights), axis=1, keepdims=True)
        acc = jnp.zeros((shard, HD), f32)
        for b in range(blocks):
            acc += jnp.dot(weights[b].astype(bf16), kv_refs[b][shard:, g * HD : (g + 1) * HD], preferred_element_type=f32)
        pieces.append(acc / total)
    stream = (res_ref[...].astype(f32) + jnp.concatenate(pieces, axis=1)).astype(bf16)
    stream_ref[...] = stream
    tn = (((0,), (0,)), ((), ()))
    send = lax.dot_general(taken_ref[...], stream, tn, preferred_element_type=f32).astype(bf16)
    for ref, (at, rows, extra) in zip(send_refs, layout):
        ref[:rows] = send[at : at + rows]
        if extra is not None:
            ref[rows:] = extra_refs[extra][...]


def joined(refs, spans):
    parts = [refs[i][at : at + rows] for i, at, rows in spans]
    return parts[0] if len(parts) == 1 else jnp.concatenate(parts, axis=0)


def whole(ref, row, width):
    return sum(ref[row + i : row + i + 1, :width].astype(f32) for i in range(3))


def load_body(*refs):
    n = len(refs) // 2
    sems = refs[-1]
    copies = [pltpu.make_async_copy(refs[i], refs[n + i], sems.at[i]) for i in range(n)]
    for c in copies:
        c.start()
    for c in copies:
        c.wait()


def load(arrays):
    n = len(arrays)
    return kernel(
        load_body, [pltpu.VMEM(a.shape, a.dtype) for a in arrays], [RAW] * n, [VMEM] * n, 4,
        scratch=[pltpu.SemaphoreType.DMA((n,))],
    )(*[pltpu.with_memory_space_constraint(a, pltpu.HBM) for a in arrays])


def join_body(first_ref, second_ref, out_ref):
    rows = first_ref.shape[0]
    out_ref[:rows] = first_ref[...]
    out_ref[rows:] = second_ref[...]


def join(first, second):
    rows = first.shape[0] + second.shape[0]
    return kernel(join_body, pltpu.VMEM((rows, first.shape[1]), first.dtype), [VMEM] * 2, VMEM, 4)(first, second)


def mlp_body(spec, lit_of, cut, begun, where_ref, *refs):
    refs = list(refs)
    acc_in = [refs.pop(0) for _ in range(3)] if begun else None
    blocks = [([refs.pop(0) for _ in range(n)], spans, gain, i) for n, spans, gain, i in spec]
    lits = [refs.pop(0) for _ in lit_of]
    gates, ups = ([refs.pop(0) for _ in range(2)] for _ in range(2))
    mine = where_ref[0]
    g, u, squares = ([None, None], [None, None], None)
    if begun:
        hidden = gates[0].shape[1]
        g = [acc_in[0][:, k * hidden : (k + 1) * hidden] for k in range(2)]
        u = [acc_in[1][:, k * hidden : (k + 1) * hidden] for k in range(2)]
        squares = acc_in[2][:, :1]

    def plus(x, y):
        return y if x is None else x + y

    for arrays, spans, gain_row, i in blocks:
        at = mine ^ i
        wide = joined(arrays, spans).astype(f32)
        quarter = wide.shape[1]
        squares = plus(squares, jnp.sum(wide * wide, axis=1, keepdims=True))
        x = (wide * whole(arrays[0], gain_row, quarter)).astype(bf16)
        part = pl.ds(pl.multiple_of(at * quarter, quarter), quarter)
        for k in range(2):
            g[k] = plus(g[k], jnp.dot(x, gates[k][part, :], preferred_element_type=f32))
            u[k] = plus(u[k], jnp.dot(x, ups[k][part, :], preferred_element_type=f32))
    if not lit_of:
        g_ref, u_ref, s_ref = refs
        g_ref[...] = jnp.concatenate(g, axis=1)
        u_ref[...] = jnp.concatenate(u, axis=1)
        s_ref[...] = jnp.broadcast_to(squares, s_ref.shape)
        return
    downs = [refs.pop(0) for _ in range(2)]
    outs = [[refs.pop(0) for _ in range(n)] for n in (cut, 1, 1, 1)]
    quarter = outs[1][0].shape[1]
    opened = [as_column(whole(ref, row, n)) for ref, (row, n) in zip(lits, lit_of)]
    opened = opened[0] if len(opened) == 1 else jnp.concatenate(opened, axis=0)
    factor = lax.rsqrt(squares / (len(outs) * quarter) + norm_eps) * opened
    act = []
    for k in range(2):
        gate, up = g[k] * factor, u[k] * factor
        act.append((gate / (1.0 + jnp.exp(-gate)) * up).astype(bf16))
    for i in (2, 1, 3, 0):
        at = mine ^ i
        part = pl.ds(pl.multiple_of(at * quarter, quarter), quarter)
        y = jnp.dot(act[0], downs[0][:, part], preferred_element_type=f32)
        y += jnp.dot(act[1], downs[1][:, part], preferred_element_type=f32)
        y = y.astype(bf16)
        top = 0
        for ref in outs[i]:
            ref[...] = y[top : top + ref.shape[0]]
            top += ref.shape[0]


def mlp(mine, blocks, weights, cut=1, begun=None, lits=()):
    spec = [(len(arrays), spans, gain, i) for arrays, spans, gain, i in blocks]
    rows, quarter = sum(n for _, _, n in blocks[0][1]), blocks[0][0][0].shape[1]
    flat = [*(begun or ()), *[a for arrays, *_ in blocks for a in arrays], *[a for a, _, _ in lits]]
    hidden = weights[0].shape[1]
    flops = 2 * rows * quarter * len(blocks) * hidden * 4
    if lits:
        out = [pltpu.VMEM((rows // cut, quarter), bf16)] * cut + [pltpu.VMEM((rows, quarter), bf16)] * 3
        flops += 2 * rows * quarter * 4 * hidden * 2
    else:
        out = [pltpu.VMEM((rows, 2 * hidden), f32)] * 2 + [pltpu.VMEM((rows, HD), f32)]
        weights = weights[:4]
    weights = [pltpu.with_memory_space_constraint(w, pltpu.VMEM) for w in weights]
    out = kernel(
        functools.partial(mlp_body, spec, [(row, n) for _, row, n in lits], cut, begun is not None),
        out,
        [SMEM] + [VMEM] * (len(flat) + len(weights)),
        [VMEM] * len(out),
        12,
        cost=pl.CostEstimate(flops=flops, bytes_accessed=8 << 20, transcendentals=0),
    )(mine, *flat, *weights)
    return (out[:cut], *out[cut:]) if lits else out


def add(*parts):
    total = parts[0].astype(f32)
    for part in parts[1:]:
        total = total + part.astype(f32)
    return total.astype(bf16)


def final_body(shape, stream_ref, taken_ref, *refs):
    refs = list(refs)
    out_ref = refs.pop()
    total = stream_ref[...].astype(f32)
    at = 0
    for n in shape:
        part = refs.pop(0)[...].astype(f32)
        for _ in range(n - 1):
            part += refs.pop(0)[...].astype(f32)
        rows = part.shape[0]
        total += jnp.dot(taken_ref[:, at : at + rows], part.astype(bf16), preferred_element_type=f32)
        at += rows
    out_ref[0] = total.astype(bf16)


def body(
    query_proj,
    key_proj,
    value_proj,
    residual,
    norm_gain,
    router_logit,
    expert_ids,
    gate_weight,
    up_weight,
    down_weight,
):
    shard, quarter = query_proj.shape[1:]
    seq, experts = lax.axis_size("seq"), lax.axis_size("exp")
    sid = lax.axis_index("seq").astype(jnp.int32)[None]
    eid = lax.axis_index("exp").astype(jnp.int32)[None]
    fid = lax.axis_index("ff").astype(jnp.int32)[None]
    cap = max(2, 3 * shard // (2 * experts))
    slots = experts * cap
    two = experts == 2
    like = jax.ShapeDtypeStruct

    def far_off(x):
        return pltpu.with_memory_space_constraint(x, pltpu.HBM)

    dma = pltpu.SemaphoreType.DMA
    near = pltpu.VMEM
    kv = kernel(
        pack_body, near((2 * shard, key_proj.shape[2]), bf16), [RAW] * 2, VMEM, 4, scratch=[dma((2,))],
    )(far_off(key_proj), far_off(value_proj))
    kv2 = flip(kv, later=True, seq=2)
    kv1 = flip(kv, later=True, seq=1)
    extras = 2 if two else 1
    query, res, taken, *extra, lit = kernel(
        functools.partial(prep_body, experts, cap),
        (
            near((shard, quarter), bf16),
            near((shard, quarter), bf16),
            near((shard, slots), bf16),
            *[near((EXTRA, quarter), bf16)] * extras,
            near((1, slots), f32),
        ),
        [SMEM] + [RAW] * 5,
        (VMEM,) * (4 + extras),
        8,
        scratch=[near((1, shard), jnp.int32), near((1, shard), f32), near((quarter,), f32), dma((5,))],
    )(eid, far_off(query_proj), far_off(residual), far_off(expert_ids[0, :, 0][None]), far_off(router_logit), far_off(norm_gain))
    kv3 = flip(kv2, seq=1)

    layout = [(0, cap, 0), (cap, cap, 1), (cap, cap, None)] if two else [(0, slots, None)]
    stream, *send = kernel(
        functools.partial(attend_body, HEADS // KVH, seq, extras, layout),
        [near((shard, quarter), bf16)] + [near((n + (0 if e is None else EXTRA), quarter), bf16) for _, n, e in layout],
        [SMEM] + [VMEM] * (3 + seq + extras),
        (VMEM,) * (1 + len(layout)),
        8,
    )(sid, query, res, taken, kv, kv1, kv2, kv3, *extra)

    weights = (gate_weight[0], up_weight[0], down_weight[0])
    tied, send = lax.optimization_barrier((weights, send))
    if two:
        mine, other, bare = send
        sel = join(flip(mine, ff=3), flip(bare, exp=1, ff=3))
        non = join(flip(mine, ff=1), flip(bare, exp=1, ff=1))
        own = [mine, flip(other, exp=1)]
        own_x = [flip(mine, seq=2), flip(other, seq=2, exp=1)]
        far_x = [flip(own_x[0], ff=2), flip(own_x[1], ff=2)]
        one = ((0, 0, cap), (0, cap + EXTRA, cap)), cap
        both = ((0, 0, cap), (1, 0, cap)), cap
        lit_of = ((cap + 3, cap), (cap + 3, cap))
        cut = 2
    else:
        block = lax.all_to_all(send[0], "exp", split_axis=0, concat_axis=0, tiled=True)
        lit = lax.all_to_all(lit[0], "exp", split_axis=0, concat_axis=0, tiled=True)
        lit = jnp.pad(jnp.stack(split(lit)), ((0, 0), (0, quarter - slots)))
        tail = jnp.concatenate([extra[0][:3], lit, extra[0][6:]], axis=0)
        block = jnp.concatenate([block, tail], axis=0)
        own, own_x = [block], [flip(block, seq=2)]
        sel, non = flip(block, ff=3), flip(block, ff=1)
        one = both = ((0, 0, slots),), slots
        far_x = [flip(own_x[0], ff=2)]
        lit_of = ((slots + 3, slots),)
        cut = 1
    partner = [flip(w, seq=1) for w in tied]
    pairs = [w for each in zip(load(weights), load(partner)) for w in each]
    far = flip(sel, ff=1)
    sel_x = flip(sel, seq=2)
    non_x = flip(non, seq=2)

    def lit_in(arrays):
        return [(a, row, n) for a, (row, n) in zip(arrays, lit_of)]

    begun = mlp(fid, [(own, *both, 0), ([sel], *one, 3), ([non], *one, 1)], pairs)
    p0, p1, p2, p3 = mlp(fid, [([far], *one, 2)], pairs, cut, begun, lit_in(own))
    begun = mlp(fid, [(own_x, *both, 0), (far_x, *both, 2), ([sel_x], *one, 3)], pairs)
    o0, o1, o2, o3 = mlp(fid, [([non_x], *one, 1)], pairs, cut, begun, lit_in(own_x))

    back_x = flip(o2, ff=1)
    back = flip(p2, ff=1)
    tot_non = add(p1, flip(o1, seq=2))
    tot_sel = add(p3, back, flip(add(o3, back_x), seq=2))
    if two:
        parts = [
            p0[0], flip(o0[0], seq=2), flip(tot_non[:cap], ff=1), flip(tot_sel[:cap], ff=3),
            flip(p0[1], exp=1), flip(o0[1], seq=2, exp=1),
            flip(tot_non[cap:], exp=1, ff=1), flip(tot_sel[cap:], exp=1, ff=3),
        ]
        shape = (4, 4)
    else:
        parts = add(p0[0], flip(o0[0], seq=2), flip(tot_non, ff=1), flip(tot_sel, ff=3))
        parts = [lax.all_to_all(parts, "exp", split_axis=0, concat_axis=0, tiled=True)]
        shape = (1,)
    return kernel(
        functools.partial(final_body, shape), like((1, shard, quarter), bf16), [VMEM] * (2 + len(parts)), VMEM, 8
    )(stream, taken, *parts)


def solution(mesh):
    placed = (
        P("exp", "seq", "ff"),
        P("exp", "seq", "ff"),
        P("exp", "seq", "ff"),
        P("exp", "seq", "ff"),
        P("ff"),
        P("exp", "seq"),
        P("exp", "seq", None),
        P("exp", None, ("seq", "ff")),
        P("exp", None, ("seq", "ff")),
        P("exp", ("seq", "ff"), None),
    )

    return jax.shard_map(body, mesh=mesh, in_specs=placed, out_specs=P("exp", "seq", "ff"), check_vma=False)
```

time: 189 us -> 88.7 us (0.47)
  waiting for transfers between devices: 113 us -> 21 us
  starting transfers between devices: 7.66 us -> 48.3 us
  blocking collectives: 28.8 us -> 0 us
  matrix products: 17.9 us -> 0 us
  Pallas kernels: 0 us -> 16.9 us
  between operations: 13.6 us -> 0.25 us
  local copies, waits for them, and re-layouts: 5.21 us -> 1.17 us
    reduce_scatter x1 -> x0, waiting for transfers between devices: 69.2 us -> none  [body(): lax.psum_scatter(term.reshape(-1, quarter).astype(jnp.bfloat16), ('seq',...]
    all_gather x1 -> x0, waiting for transfers between devices: 43.7 us -> none  [body(): everyone = lax.all_gather(incoming, ('seq', 'ff'), axis=0, tiled=True)]
    ppermute x3 -> x29, starting transfers between devices: 7.62 us -> 48.3 us  [flip(): return lax.ppermute(value, axes, pairs)]
    ppermute x3 -> x29, waiting for transfers between devices: 0.01 us -> 21 us  [flip(): return lax.ppermute(value, axes, pairs)]
    dot_general x13 -> x0, matrix products: 17.9 us -> none  [the longest x1 8.36 us: body(): jnp.einsum('sjk,kfc->sfjc', activated, down_parts, preferred_element_type...]
    pallas_call x0 -> x12, Pallas kernels: none -> 16.9 us  [the longest x4 7.1 us: mlp(): kernel(functools.partial(mlp_body, spec, [(row, n) for _, row, n in lits]...]
    all_to_all x2 -> x0, blocking collectives: 16.7 us -> none  [the longest x1 8.51 us: body(): lax.all_to_all(summed, 'exp', split_axis=0, concat_axis=0, tiled=True)]
    psum x1 -> x0, blocking collectives: 12.1 us -> none  [body(): squares = lax.psum(jnp.sum(stream_f * stream_f, axis=1), 'ff')]
  transfers between devices with their start and end apart: 5 -> 29, of which waited for: 2 -> 9; matrix products, arithmetic and copies ran while one was open for 4% -> 0% of each run, Pallas kernels for 0% -> 15%
where the time goes in v1:
time: 88.7 us; the launch traced here: 87.8 us
  starting transfers between devices  48.3 us (54%)
  waiting for transfers between devices  21 us (24%)
  Pallas kernels  16.9 us (19%)
  local copies, waits for them, and re-layouts  1.17 us (1%)
    ppermute x29, starting transfers between devices, flip(): return lax.ppermute(value, axes, pairs)  48.3 us
    ppermute x29, waiting for transfers between devices, flip(): return lax.ppermute(value, axes, pairs)  21 us
    pallas_call x4, Pallas kernels, mlp(): kernel(functools.partial(mlp_body, spec, [(row, n) for _, row, n in lits]...  7.1 us
    pallas_call x2, Pallas kernels, load(): kernel(load_body, [pltpu.VMEM(a.shape, a.dtype) for a in arrays], [RAW] *...  4.26 us
    pallas_call x1, Pallas kernels, body(): kernel(functools.partial(attend_body, HEADS // KVH, seq, extras, layout),...  1.92 us
    pallas_call x1, Pallas kernels, body(): kernel(functools.partial(prep_body, experts, cap), (near((shard, quarter)...  1.78 us
  transfers between devices with their start and end apart: 29, of which 9 were waited for; matrix products, arithmetic and copies ran while one was open for 0% of the time, Pallas kernels for 15%

profile of v1, /device:TPU:0, one launch (start us, length us, event | category | flops | bytes accessed | tf_op | source)
XLA Modules:
  0.0 87.8 jit_solution(13283291795738118006)
XLA Ops:
  0.8 4.9 %collective-permute-start.1 = (bf16[256,128]{1,0:T(8,128)(2,1)S(1)}, bf16[256,128]{1,0:T(8,128)(2,1)S(1)}, u32[]{:S(2)}, u32[]{:S(2)}) collective-permute-start(bf16[256,128]{1,0:T(8,128)(2,1)S(1)} %shard_map.101.refs_0_), channel_id=1, source_target_pairs={{0,16},{8,24},{1,17},{9,25},{2,18},{10,26},{3,19},{11,27},{4,20},{... | collective-permute-start | bytes 196616 | tf_op jit(solution)/shard_map/ppermute | solution.py:51
  7.6 1.8 %shard_map.100 = (bf16[128,640]{1,0:T(8,128)(2,1)S(1)}, bf16[128,640]{1,0:T(8,128)(2,1)S(1)}, bf16[128,192]{1,0:T(8,128)(2,1)S(1)}, bf16[16,640]{1,0:T(8,128)(2,...) custom-call(s32[1]{0:T(128)} %bitcast.1.where_ref, bf16[1,128,640]{2,1,0:T(8,128)(2,1)} %q_in.1, ...), custom_call_target="tpu_custom_call" | custom-call | tf_op jit(solution)/shard_map/pallas_call | solution.py:328
  9.4 1.9 %shard_map.102 = (bf16[128,640]{1,0:T(8,128)(2,1)S(1)}, bf16[112,640]{1,0:T(8,128)(2,1)S(1)}, bf16[112,640]{1,0:T(8,128)(2,1)S(1)}, bf16[96,640]{1,0:T(8,128)(2,1)S(1)}) custom-call(s32[1]{0:T(128)} %bitcast.where_ref, bf16[128,640]{1,0:T(8,128)(2,1)S(1)} %get-tuple-element.42.q_ref, bf16[128,640]{1,0:T(8,128)(2,1)S(1)} %get-tuple-element.43.res_ref, ...), custom_call_target="tpu_custom_call" | custom-call | tf_op jit(solution)/shard_map/pallas_call | solution.py:345
  12.4 4.6 %collective-permute-start.5 = (bf16[96,640]{1,0:T(8,128)(2,1)S(1)}, bf16[96,640]{1,0:T(8,128)(2,1)S(1)}, u32[]{:S(2)}, u32[]{:S(2)}) collective-permute-start(bf16[96,640]{1,0:T(8,128)(2,1)S(1)} %get-tuple-element.53), channel_id=1, source_target_pairs={{0,7},{1,6},{2,5},{3,4},{4,3},{5,2},{6,1},{7,0},{8,15},{9,14},{10,... | collective-permute-start | bytes 368648 | tf_op jit(solution)/shard_map/ppermute | solution.py:51
  17.0 4.4 %collective-permute-done.5.second_ref = bf16[96,640]{1,0:T(8,128)(2,1)S(1)} collective-permute-done((bf16[96,640]{1,0:T(8,128)(2,1)S(1)}, bf16[96,640]{1,0:T(8,128)(2,1)S(1)}, u32[]{:S(2)}, u32[]{:S(2)}) %collective-permute-start.5) | collective-permute-done | bytes 122912 | tf_op jit(solution)/shard_map/ppermute | solution.py:51
  21.4 3.6 %collective-permute-start.4 = (bf16[112,640]{1,0:T(8,128)(2,1)S(1)}, bf16[112,640]{1,0:T(8,128)(2,1)S(1)}, u32[]{:S(2)}, u32[]{:S(2)}) collective-permute-start(bf16[112,640]{1,0:T(8,128)(2,1)S(1)} %get-tuple-element.51.refs_0_.refs_4_), channel_id=1, source_target_pairs={{0,3},{1,2},{2,1},{3,0},{4,7},{5,6},{6,5},{7,4},{8,11},{9,10},{10,... | collective-permute-start | bytes 430088 | tf_op jit(solution)/shard_map/ppermute | solution.py:51
  25.0 2.4 %collective-permute-start.12 = (bf16[112,640]{1,0:T(8,128)(2,1)S(1)}, bf16[112,640]{1,0:T(8,128)(2,1)S(1)}, u32[]{:S(2)}, u32[]{:S(2)}) collective-permute-start(bf16[112,640]{1,0:T(8,128)(2,1)S(1)} %get-tuple-element.51.refs_0_.refs_4_), channel_id=1, source_target_pairs={{0,16},{8,24},{16,0},{24,8},{1,17},{9,25},{17,1},{25,9},{2,18},{10... | collective-permute-start | bytes 430088 | tf_op jit(solution)/shard_map/ppermute | solution.py:51
  28.4 2.4 %collective-permute-start.6 = (bf16[112,640]{1,0:T(8,128)(2,1)S(1)}, bf16[112,640]{1,0:T(8,128)(2,1)S(1)}, u32[]{:S(2)}, u32[]{:S(2)}) collective-permute-start(bf16[112,640]{1,0:T(8,128)(2,1)S(1)} %get-tuple-element.51.refs_0_.refs_4_), channel_id=1, source_target_pairs={{0,1},{1,0},{2,3},{3,2},{4,5},{5,4},{6,7},{7,6},{8,9},{9,8},{10,11... | collective-permute-start | bytes 430088 | tf_op jit(solution)/shard_map/ppermute | solution.py:51
  30.8 3.3 %collective-permute-start.13 = (bf16[112,640]{1,0:T(8,128)(2,1)S(1)}, bf16[112,640]{1,0:T(8,128)(2,1)}, u32[]{:S(2)}, u32[]{:S(2)}) collective-permute-start(bf16[112,640]{1,0:T(8,128)(2,1)S(1)} %get-tuple-element.52), channel_id=1, source_target_pairs={{0,20},{4,16},{8,28},{12,24},{16,4},{20,0},{24,12},{28,8},{1,21},{... | collective-permute-start | bytes 430088 | tf_op jit(solution)/shard_map/ppermute | solution.py:51
  34.2 2.4 %collective-permute-start.16 = (bf16[208,640]{1,0:T(8,128)(2,1)S(1)}, bf16[208,640]{1,0:T(8,128)(2,1)}, u32[]{:S(2)}, u32[]{:S(2)}) collective-permute-start(bf16[208,640]{1,0:T(8,128)(2,1)S(1)} %shard_map.103.refs_2_), channel_id=1, source_target_pairs={{0,16},{8,24},{16,0},{24,8},{1,17},{9,25},{17,1},{25,9},{2,18},{10... | collective-permute-start | bytes 798728 | tf_op jit(solution)/shard_map/ppermute | solution.py:51
  39.5 3.1 %collective-permute-start.14 = (bf16[112,640]{1,0:T(8,128)(2,1)S(1)}, bf16[112,640]{1,0:T(8,128)(2,1)}, u32[]{:S(2)}, u32[]{:S(2)}) collective-permute-start(bf16[112,640]{1,0:T(8,128)(2,1)S(1)} %collective-permute-done.12.refs_0_.refs_4_), channel_id=1, source_target_pairs={{0,2},{1,3},{2,0},{3,1},{4,6},{5,7},{6,4},{7,5},{8,10},{9,11},{10,... | collective-permute-start | bytes 430088 | tf_op jit(solution)/shard_map/ppermute | solution.py:51
  43.7 2.1 %shard_map.105 = (bf16[2560,256]{1,0:T(8,128)(2,1)S(1)}, bf16[2560,256]{1,0:T(8,128)(2,1)S(1)}, bf16[256,2560]{1,0:T(8,128)(2,1)S(1)}) custom-call(bf16[2560,256]{1,0:T(8,128)(2,1)} %bitcast.8, bf16[2560,256]{1,0:T(8,128)(2,1)} %bitcast.12, bf16[256,2560]{1,0:T(8,128)(2,1)} %bitcast.10), custom_call_target="tpu_custom_call" | custom-call | tf_op jit(solution)/shard_map/pallas_call | solution.py:177
  46.9 1.5 %collective-permute-start.3 = (bf16[112,640]{1,0:T(8,128)(2,1)}, bf16[112,640]{1,0:T(8,128)(2,1)S(1)}, u32[]{:S(2)}, u32[]{:S(2)}) collective-permute-start(bf16[112,640]{1,0:T(8,128)(2,1)} %copy-done.4), channel_id=1, source_target_pairs={{0,4},{4,0},{1,5},{5,1},{2,6},{6,2},{3,7},{7,3},{8,12},{12,8},{9,1... | collective-permute-start | bytes 430088 | tf_op jit(solution)/shard_map/ppermute | solution.py:51
  48.4 2.1 %shard_map.106 = (bf16[2560,256]{1,0:T(8,128)(2,1)S(1)}, bf16[2560,256]{1,0:T(8,128)(2,1)S(1)}, bf16[256,2560]{1,0:T(8,128)(2,1)S(1)}) custom-call(bf16[2560,256]{1,0:T(8,128)(2,1)} %copy-done.6, bf16[2560,256]{1,0:T(8,128)(2,1)} %collective-permute-done.9.refs_1_, bf16[256,2560]{1,0:T(8,128)(2,1)} %copy-done.5), custom_call_target="tpu_custom_call" | custom-call | tf_op jit(solution)/shard_map/pallas_call | solution.py:177
  51.5 1.5 %collective-permute-done.15.refs_3_ = bf16[112,640]{1,0:T(8,128)(2,1)} collective-permute-done((bf16[112,640]{1,0:T(8,128)(2,1)}, bf16[112,640]{1,0:T(8,128)(2,1)}, u32[]{:S(2)}, u32[]{:S(2)}) %collective-permute-start.15) | collective-permute-done | bytes 143392 | tf_op jit(solution)/shard_map/ppermute | solution.py:51
  53.0 2.4 %shard_map.109 = (f32[192,512]{1,0:T(8,128)S(1)}, f32[192,512]{1,0:T(8,128)S(1)}, f32[192,128]{1,0:T(8,128)S(1)}) custom-call(s32[1]{0:T(128)} %bitcast.3.where_ref, bf16[112,640]{1,0:T(8,128)(2,1)S(1)} %collective-permute-done.12.refs_0_.refs_4_, bf16[112,640]{1,0:T(8,128)(2,1)} %collective-permute-done.13.refs_1_.refs_5_, ...), custom_call_target="tpu_custom_call" | custom-call | flops 754974720 | bytes 8388608 | tf_op jit(solution)/shard_map/pallas_call | solution.py:262
  55.4 2.3 %shard_map.110 = (bf16[96,640]{1,0:T(8,128)(2,1)S(1)}, bf16[96,640]{1,0:T(8,128)(2,1)S(1)}, bf16[192,640]{1,0:T(8,128)(2,1)S(1)}, bf16[192,640]{1,0:T(8,128)(2,1)S(1)}, bf16[192,640]{1,0:T(8,128)(2,1)S(1)}) custom-call(s32[1]{0:T(128)} %bitcast.3.where_ref, f32[192,512]{1,0:T(8,128)S(1)} %get-tuple-element.67.refs_0_, ...), custom_call_target="tpu_custom_call" | custom-call | flops 754974720 | bytes 8388608 | tf_op jit(solution)/shard_map/pallas_call | solution.py:262
  60.9 2.0 %collective-permute-start.21 = (bf16[192,640]{1,0:T(8,128)(2,1)S(1)}, bf16[192,640]{1,0:T(8,128)(2,1)S(1)}, u32[]{:S(2)}, u32[]{:S(2)}) collective-permute-start(bf16[192,640]{1,0:T(8,128)(2,1)S(1)} %get-tuple-element.74), channel_id=1, source_target_pairs={{0,1},{1,0},{2,3},{3,2},{4,5},{5,4},{6,7},{7,6},{8,9},{9,8},{10,11... | collective-permute-start | bytes 737288 | tf_op jit(solution)/shard_map/ppermute | solution.py:51
  66.6 1.5 %collective-permute-start.25 = (bf16[96,640]{1,0:T(8,128)(2,1)S(1)}, bf16[96,640]{1,0:T(8,128)(2,1)S(1)}, u32[]{:S(2)}, u32[]{:S(2)}) collective-permute-start(bf16[96,640]{1,0:T(8,128)(2,1)S(1)} %get-tuple-element.77), channel_id=1, source_target_pairs={{0,4},{4,0},{1,5},{5,1},{2,6},{6,2},{3,7},{7,3},{8,12},{12,8},{9,1... | collective-permute-start | bytes 368648 | tf_op jit(solution)/shard_map/ppermute | solution.py:51
  68.7 1.7 %collective-permute-done.21 = bf16[192,640]{1,0:T(8,128)(2,1)S(1)} collective-permute-done((bf16[192,640]{1,0:T(8,128)(2,1)S(1)}, bf16[192,640]{1,0:T(8,128)(2,1)S(1)}, u32[]{:S(2)}, u32[]{:S(2)}) %collective-permute-start.21) | collective-permute-done | bytes 245792 | tf_op jit(solution)/shard_map/ppermute | solution.py:51
  70.7 5.1 %collective-permute-done.23 = bf16[192,640]{1,0:T(8,128)(2,1)S(1)} collective-permute-done((bf16[192,640]{1,0:T(8,128)(2,1)S(1)}, bf16[192,640]{1,0:T(8,128)(2,1)S(1)}, u32[]{:S(2)}, u32[]{:S(2)}) %collective-permute-start.23) | collective-permute-done | bytes 245792 | tf_op jit(solution)/shard_map/ppermute | solution.py:51
  75.7 2.2 %collective-permute-start.27 = (bf16[96,640]{1,0:T(8,128)(2,1)S(1)}, bf16[96,640]{1,0:T(8,128)(2,1)S(1)}, u32[]{:S(2)}, u32[]{:S(2)}) collective-permute-start(bf16[96,640]{1,0:T(8,128)(2,1)S(1)} %get-tuple-element.81), channel_id=1, source_target_pairs={{0,5},{1,4},{2,7},{3,6},{4,1},{5,0},{6,3},{7,2},{8,13},{9,12},{10,... | collective-permute-start | bytes 368648 | tf_op jit(solution)/shard_map/ppermute | solution.py:51
  78.4 4.0 %collective-permute-start.28 = (bf16[96,640]{1,0:T(8,128)(2,1)S(1)}, bf16[96,640]{1,0:T(8,128)(2,1)S(1)}, u32[]{:S(2)}, u32[]{:S(2)}) collective-permute-start(bf16[96,640]{1,0:T(8,128)(2,1)S(1)} %get-tuple-element.79), channel_id=1, source_target_pairs={{0,7},{1,6},{2,5},{3,4},{4,3},{5,2},{6,1},{7,0},{8,15},{9,14},{10,... | collective-permute-start | bytes 368648 | tf_op jit(solution)/shard_map/ppermute | solution.py:51
  82.4 4.4 %collective-permute-done.27.refs_6_ = bf16[96,640]{1,0:T(8,128)(2,1)S(1)} collective-permute-done((bf16[96,640]{1,0:T(8,128)(2,1)S(1)}, bf16[96,640]{1,0:T(8,128)(2,1)S(1)}, u32[]{:S(2)}, u32[]{:S(2)}) %collective-permute-start.27) | collective-permute-done | bytes 122912 | tf_op jit(solution)/shard_map/ppermute | solution.py:51
  (65 shorter events, 19.9 us)
Async XLA Ops:
  11.3 28.1 %collective-permute-start.10 = (bf16[256,2560]{1,0:T(8,128)(2,1)}, bf16[256,2560]{1,0:T(8,128)(2,1)S(1)}, u32[]{:S(2)}, u32[]{:S(2)}) collective-permute-start(bf16[256,2560]{1,0:T(8,128)(2,1)} %bitcast.9), channel_id=1, source_target_pairs={{0,8},{8,0},{16,24},{24,16},{1,9},{9,1},{17,25},{25,17},{2,10},{10... | collective-permute-start | bytes 3932168 | tf_op jit(solution)/shard_map/ppermute | solution.py:51
  11.9 30.7 %collective-permute-start.8 = (bf16[2560,256]{1,0:T(8,128)(2,1)}, bf16[2560,256]{1,0:T(8,128)(2,1)S(1)}, u32[]{:S(2)}, u32[]{:S(2)}) collective-permute-start(bf16[2560,256]{1,0:T(8,128)(2,1)} %bitcast.7), channel_id=1, source_target_pairs={{0,8},{8,0},{16,24},{24,16},{1,9},{9,1},{17,25},{25,17},{2,10},{10... | collective-permute-start | bytes 3932168 | tf_op jit(solution)/shard_map/ppermute | solution.py:51
  12.0 34.9 %collective-permute-start.9 = (bf16[2560,256]{1,0:T(8,128)(2,1)}, bf16[2560,256]{1,0:T(8,128)(2,1)}, u32[]{:S(2)}, u32[]{:S(2)}) collective-permute-start(bf16[2560,256]{1,0:T(8,128)(2,1)} %bitcast.11), channel_id=1, source_target_pairs={{0,8},{8,0},{16,24},{24,16},{1,9},{9,1},{17,25},{25,17},{2,10},{10... | collective-permute-start | bytes 3932168 | tf_op jit(solution)/shard_map/ppermute | solution.py:51
  12.4 8.9 %collective-permute-start.5 = (bf16[96,640]{1,0:T(8,128)(2,1)S(1)}, bf16[96,640]{1,0:T(8,128)(2,1)S(1)}, u32[]{:S(2)}, u32[]{:S(2)}) collective-permute-start(bf16[96,640]{1,0:T(8,128)(2,1)S(1)} %get-tuple-element.53), channel_id=1, source_target_pairs={{0,7},{1,6},{2,5},{3,4},{4,3},{5,2},{6,1},{7,0},{8,15},{9,14},{10,... | collective-permute-start | bytes 368648 | tf_op jit(solution)/shard_map/ppermute | solution.py:51
  17.0 8.0 %collective-permute-start.7 = (bf16[96,640]{1,0:T(8,128)(2,1)S(1)}, bf16[96,640]{1,0:T(8,128)(2,1)S(1)}, u32[]{:S(2)}, u32[]{:S(2)}) collective-permute-start(bf16[96,640]{1,0:T(8,128)(2,1)S(1)} %get-tuple-element.53), channel_id=1, source_target_pairs={{0,5},{1,4},{2,7},{3,6},{4,1},{5,0},{6,3},{7,2},{8,13},{9,12},{10,... | collective-permute-start | bytes 368648 | tf_op jit(solution)/shard_map/ppermute | solution.py:51
  21.4 7.0 %collective-permute-start.4 = (bf16[112,640]{1,0:T(8,128)(2,1)S(1)}, bf16[112,640]{1,0:T(8,128)(2,1)S(1)}, u32[]{:S(2)}, u32[]{:S(2)}) collective-permute-start(bf16[112,640]{1,0:T(8,128)(2,1)S(1)} %get-tuple-element.51.refs_0_.refs_4_), channel_id=1, source_target_pairs={{0,3},{1,2},{2,1},{3,0},{4,7},{5,6},{6,5},{7,4},{8,11},{9,10},{10,... | collective-permute-start | bytes 430088 | tf_op jit(solution)/shard_map/ppermute | solution.py:51
  30.8 7.2 %collective-permute-start.13 = (bf16[112,640]{1,0:T(8,128)(2,1)S(1)}, bf16[112,640]{1,0:T(8,128)(2,1)}, u32[]{:S(2)}, u32[]{:S(2)}) collective-permute-start(bf16[112,640]{1,0:T(8,128)(2,1)S(1)} %get-tuple-element.52), channel_id=1, source_target_pairs={{0,20},{4,16},{8,28},{12,24},{16,4},{20,0},{24,12},{28,8},{1,21},{... | collective-permute-start | bytes 430088 | tf_op jit(solution)/shard_map/ppermute | solution.py:51
  34.2 18.8 %collective-permute-start.16 = (bf16[208,640]{1,0:T(8,128)(2,1)S(1)}, bf16[208,640]{1,0:T(8,128)(2,1)}, u32[]{:S(2)}, u32[]{:S(2)}) collective-permute-start(bf16[208,640]{1,0:T(8,128)(2,1)S(1)} %shard_map.103.refs_2_), channel_id=1, source_target_pairs={{0,16},{8,24},{16,0},{24,8},{1,17},{9,25},{17,1},{25,9},{2,18},{10... | collective-permute-start | bytes 798728 | tf_op jit(solution)/shard_map/ppermute | solution.py:51
  38.0 17.4 %collective-permute-start.17 = (bf16[208,640]{1,0:T(8,128)(2,1)S(1)}, bf16[208,640]{1,0:T(8,128)(2,1)}, u32[]{:S(2)}, u32[]{:S(2)}) collective-permute-start(bf16[208,640]{1,0:T(8,128)(2,1)S(1)} %shard_map.104.refs_3_), channel_id=1, source_target_pairs={{0,16},{8,24},{16,0},{24,8},{1,17},{9,25},{17,1},{25,9},{2,18},{10... | collective-permute-start | bytes 798728 | tf_op jit(solution)/shard_map/ppermute | solution.py:51
  39.5 11.1 %collective-permute-start.14 = (bf16[112,640]{1,0:T(8,128)(2,1)S(1)}, bf16[112,640]{1,0:T(8,128)(2,1)}, u32[]{:S(2)}, u32[]{:S(2)}) collective-permute-start(bf16[112,640]{1,0:T(8,128)(2,1)S(1)} %collective-permute-done.12.refs_0_.refs_4_), channel_id=1, source_target_pairs={{0,2},{1,3},{2,0},{3,1},{4,6},{5,7},{6,4},{7,5},{8,10},{9,11},{10,... | collective-permute-start | bytes 430088 | tf_op jit(solution)/shard_map/ppermute | solution.py:51
  42.6 10.4 %collective-permute-start.15 = (bf16[112,640]{1,0:T(8,128)(2,1)}, bf16[112,640]{1,0:T(8,128)(2,1)}, u32[]{:S(2)}, u32[]{:S(2)}) collective-permute-start(bf16[112,640]{1,0:T(8,128)(2,1)} %collective-permute-done.13.refs_1_.refs_5_), channel_id=1, source_target_pairs={{0,2},{1,3},{2,0},{3,1},{4,6},{5,7},{6,4},{7,5},{8,10},{9,11},{10,... | collective-permute-start | bytes 430088 | tf_op jit(solution)/shard_map/ppermute | solution.py:51
  46.9 11.6 %collective-permute-start.3 = (bf16[112,640]{1,0:T(8,128)(2,1)}, bf16[112,640]{1,0:T(8,128)(2,1)S(1)}, u32[]{:S(2)}, u32[]{:S(2)}) collective-permute-start(bf16[112,640]{1,0:T(8,128)(2,1)} %copy-done.4), channel_id=1, source_target_pairs={{0,4},{4,0},{1,5},{5,1},{2,6},{6,2},{3,7},{7,3},{8,12},{12,8},{9,1... | collective-permute-start | bytes 430088 | tf_op jit(solution)/shard_map/ppermute | solution.py:51
  50.5 9.0 %collective-permute-start.11 = (bf16[208,640]{1,0:T(8,128)(2,1)S(1)}, bf16[208,640]{1,0:T(8,128)(2,1)S(1)}, u32[]{:S(2)}, u32[]{:S(2)}) collective-permute-start(bf16[208,640]{1,0:T(8,128)(2,1)S(1)} %shard_map.103.refs_2_), channel_id=1, source_target_pairs={{0,1},{1,0},{2,3},{3,2},{4,5},{5,4},{6,7},{7,6},{8,9},{9,8},{10,11... | collective-permute-start | bytes 798728 | tf_op jit(solution)/shard_map/ppermute | solution.py:51
  57.7 8.9 %collective-permute-start.22 = (bf16[192,640]{1,0:T(8,128)(2,1)S(1)}, bf16[192,640]{1,0:T(8,128)(2,1)S(1)}, u32[]{:S(2)}, u32[]{:S(2)}) collective-permute-start(bf16[192,640]{1,0:T(8,128)(2,1)S(1)} %get-tuple-element.76), channel_id=1, source_target_pairs={{0,1},{1,0},{2,3},{3,2},{4,5},{5,4},{6,7},{7,6},{8,9},{9,8},{10,11... | collective-permute-start | bytes 737288 | tf_op jit(solution)/shard_map/ppermute | solution.py:51
  57.8 10.4 %collective-permute-start.19 = (bf16[192,640]{1,0:T(8,128)(2,1)S(1)}, bf16[192,640]{1,0:T(8,128)(2,1)S(1)}, u32[]{:S(2)}, u32[]{:S(2)}) collective-permute-start(bf16[192,640]{1,0:T(8,128)(2,1)S(1)} %get-tuple-element.72), channel_id=1, source_target_pairs={{0,16},{8,24},{16,0},{24,8},{1,17},{9,25},{17,1},{25,9},{2,18},{10... | collective-permute-start | bytes 737288 | tf_op jit(solution)/shard_map/ppermute | solution.py:51
  60.9 9.5 %collective-permute-start.21 = (bf16[192,640]{1,0:T(8,128)(2,1)S(1)}, bf16[192,640]{1,0:T(8,128)(2,1)S(1)}, u32[]{:S(2)}, u32[]{:S(2)}) collective-permute-start(bf16[192,640]{1,0:T(8,128)(2,1)S(1)} %get-tuple-element.74), channel_id=1, source_target_pairs={{0,1},{1,0},{2,3},{3,2},{4,5},{5,4},{6,7},{7,6},{8,9},{9,8},{10,11... | collective-permute-start | bytes 737288 | tf_op jit(solution)/shard_map/ppermute | solution.py:51
  62.9 15.2 %collective-permute-start.18 = (bf16[96,640]{1,0:T(8,128)(2,1)S(1)}, bf16[96,640]{1,0:T(8,128)(2,1)S(1)}, u32[]{:S(2)}, u32[]{:S(2)}) collective-permute-start(bf16[96,640]{1,0:T(8,128)(2,1)S(1)} %get-tuple-element.70), channel_id=1, source_target_pairs={{0,16},{8,24},{16,0},{24,8},{1,17},{9,25},{17,1},{25,9},{2,18},{10... | collective-permute-start | bytes 368648 | tf_op jit(solution)/shard_map/ppermute | solution.py:51
  64.3 14.0 %collective-permute-start.26 = (bf16[96,640]{1,0:T(8,128)(2,1)S(1)}, bf16[96,640]{1,0:T(8,128)(2,1)S(1)}, u32[]{:S(2)}, u32[]{:S(2)}) collective-permute-start(bf16[96,640]{1,0:T(8,128)(2,1)S(1)} %get-tuple-element.78), channel_id=1, source_target_pairs={{0,20},{4,16},{8,28},{12,24},{16,4},{20,0},{24,12},{28,8},{1,21},{... | collective-permute-start | bytes 368648 | tf_op jit(solution)/shard_map/ppermute | solution.py:51
  66.6 15.8 %collective-permute-start.25 = (bf16[96,640]{1,0:T(8,128)(2,1)S(1)}, bf16[96,640]{1,0:T(8,128)(2,1)S(1)}, u32[]{:S(2)}, u32[]{:S(2)}) collective-permute-start(bf16[96,640]{1,0:T(8,128)(2,1)S(1)} %get-tuple-element.77), channel_id=1, source_target_pairs={{0,4},{4,0},{1,5},{5,1},{2,6},{6,2},{3,7},{7,3},{8,12},{12,8},{9,1... | collective-permute-start | bytes 368648 | tf_op jit(solution)/shard_map/ppermute | solution.py:51
  68.2 7.6 %collective-permute-start.23 = (bf16[192,640]{1,0:T(8,128)(2,1)S(1)}, bf16[192,640]{1,0:T(8,128)(2,1)S(1)}, u32[]{:S(2)}, u32[]{:S(2)}) collective-permute-start(bf16[192,640]{1,0:T(8,128)(2,1)S(1)} %add_convert_fusion.1), channel_id=1, source_target_pairs={{0,16},{8,24},{16,0},{24,8},{1,17},{9,25},{17,1},{25,9},{2,18},{10... | collective-permute-start | bytes 737288 | tf_op jit(solution)/shard_map/ppermute | solution.py:51
  70.4 12.0 %collective-permute-start.20 = (bf16[96,640]{1,0:T(8,128)(2,1)S(1)}, bf16[96,640]{1,0:T(8,128)(2,1)S(1)}, u32[]{:S(2)}, u32[]{:S(2)}) collective-permute-start(bf16[96,640]{1,0:T(8,128)(2,1)S(1)} %get-tuple-element.82), channel_id=1, source_target_pairs={{0,1},{1,0},{2,3},{3,2},{4,5},{5,4},{6,7},{7,6},{8,9},{9,8},{10,11... | collective-permute-start | bytes 368648 | tf_op jit(solution)/shard_map/ppermute | solution.py:51
  75.7 11.0 %collective-permute-start.27 = (bf16[96,640]{1,0:T(8,128)(2,1)S(1)}, bf16[96,640]{1,0:T(8,128)(2,1)S(1)}, u32[]{:S(2)}, u32[]{:S(2)}) collective-permute-start(bf16[96,640]{1,0:T(8,128)(2,1)S(1)} %get-tuple-element.81), channel_id=1, source_target_pairs={{0,5},{1,4},{2,7},{3,6},{4,1},{5,0},{6,3},{7,2},{8,13},{9,12},{10,... | collective-permute-start | bytes 368648 | tf_op jit(solution)/shard_map/ppermute | solution.py:51
  78.1 8.7 %collective-permute-start.24 = (bf16[96,640]{1,0:T(8,128)(2,1)S(1)}, bf16[96,640]{1,0:T(8,128)(2,1)S(1)}, u32[]{:S(2)}, u32[]{:S(2)}) collective-permute-start(bf16[96,640]{1,0:T(8,128)(2,1)S(1)} %get-tuple-element.80), channel_id=1, source_target_pairs={{0,3},{1,2},{2,1},{3,0},{4,7},{5,6},{6,5},{7,4},{8,11},{9,10},{10,... | collective-permute-start | bytes 368648 | tf_op jit(solution)/shard_map/ppermute | solution.py:51
  78.4 8.4 %collective-permute-start.28 = (bf16[96,640]{1,0:T(8,128)(2,1)S(1)}, bf16[96,640]{1,0:T(8,128)(2,1)S(1)}, u32[]{:S(2)}, u32[]{:S(2)}) collective-permute-start(bf16[96,640]{1,0:T(8,128)(2,1)S(1)} %get-tuple-element.79), channel_id=1, source_target_pairs={{0,7},{1,6},{2,5},{3,4},{4,3},{5,2},{6,1},{7,0},{8,15},{9,14},{10,... | collective-permute-start | bytes 368648 | tf_op jit(solution)/shard_map/ppermute | solution.py:51
  (12 other events, 113.3 us)

commit v2 on v1

--- a/solution.py
+++ b/solution.py
@@ -32,22 +32,20 @@
     )
 
 
-def flip(value, later=False, **bits):
-    axes = tuple(bits)
-    pairs = [((), ())]
-    for axis in axes:
-        n = lax.axis_size(axis)
-        pairs = [(s + (i,), t + (i ^ bits[axis],)) for s, t in pairs for i in range(n)]
-
-    def flat(index):
-        total = 0
-        for axis, i in zip(axes, index):
-            total = total * lax.axis_size(axis) + i
-        return total
-
-    pairs = [(flat(s), flat(t)) for s, t in pairs]
-    if later:
-        pairs = [(s, t) for s, t in pairs if s < t]
+def flip(value, cross=False, later=False, seq=0, exp=0, ff=0):
+    axes = ("seq", "exp", "ff")
+    sizes = [lax.axis_size(axis) for axis in axes]
+
+    def flat(s, e, f):
+        return (s * sizes[1] + e) * sizes[2] + f
+
+    pairs = []
+    for s in range(sizes[0]):
+        for e in range(sizes[1]):
+            for f in range(sizes[2]):
+                turn = exp ^ (1 if cross and s % 2 else 0)
+                if not later or s < s ^ seq:
+                    pairs.append((flat(s, e, f), flat(s ^ seq, e ^ turn, f ^ ff)))
     return lax.ppermute(value, axes, pairs)
 
 
@@ -149,8 +147,9 @@
     send = lax.dot_general(taken_ref[...], stream, tn, preferred_element_type=f32).astype(bf16)
     for ref, (at, rows, extra) in zip(send_refs, layout):
         ref[:rows] = send[at : at + rows]
-        if extra is not None:
-            ref[rows:] = extra_refs[extra][...]
+        if extra:
+            own, got = extra_refs[0][...], extra_refs[1][...]
+            ref[rows:] = jnp.concatenate([own[:6], got[3:6], own[9:]], axis=0)
 
 
 def joined(refs, spans):
@@ -180,18 +179,14 @@
     )(*[pltpu.with_memory_space_constraint(a, pltpu.HBM) for a in arrays])
 
 
-def join_body(first_ref, second_ref, out_ref):
-    rows = first_ref.shape[0]
-    out_ref[:rows] = first_ref[...]
-    out_ref[rows:] = second_ref[...]
-
-
-def join(first, second):
-    rows = first.shape[0] + second.shape[0]
-    return kernel(join_body, pltpu.VMEM((rows, first.shape[1]), first.dtype), [VMEM] * 2, VMEM, 4)(first, second)
-
-
-def mlp_body(spec, lit_of, cut, begun, where_ref, *refs):
+def join_body(keep_ref, got_ref, out_ref):
+    cap = got_ref.shape[0]
+    out_ref[:cap] = keep_ref[:cap]
+    out_ref[cap : 2 * cap] = got_ref[...]
+    out_ref[2 * cap :] = keep_ref[cap:]
+
+
+def mlp_body(spec, lit_of, begun, where_ref, *refs):
     refs = list(refs)
     acc_in = [refs.pop(0) for _ in range(3)] if begun else None
     blocks = [([refs.pop(0) for _ in range(n)], spans, gain, i) for n, spans, gain, i in spec]
@@ -225,49 +220,50 @@
         s_ref[...] = jnp.broadcast_to(squares, s_ref.shape)
         return
     downs = [refs.pop(0) for _ in range(2)]
-    outs = [[refs.pop(0) for _ in range(n)] for n in (cut, 1, 1, 1)]
-    quarter = outs[1][0].shape[1]
+    outs = refs
+    rows, quarter = outs[0].shape
     opened = [as_column(whole(ref, row, n)) for ref, (row, n) in zip(lits, lit_of)]
     opened = opened[0] if len(opened) == 1 else jnp.concatenate(opened, axis=0)
-    factor = lax.rsqrt(squares / (len(outs) * quarter) + norm_eps) * opened
+    factor = lax.rsqrt(squares / (4 * quarter) + norm_eps) * opened
     act = []
     for k in range(2):
         gate, up = g[k] * factor, u[k] * factor
         act.append((gate / (1.0 + jnp.exp(-gate)) * up).astype(bf16))
-    for i in (2, 1, 3, 0):
+    for i in (3, 1, 2, 0):
         at = mine ^ i
         part = pl.ds(pl.multiple_of(at * quarter, quarter), quarter)
         y = jnp.dot(act[0], downs[0][:, part], preferred_element_type=f32)
         y += jnp.dot(act[1], downs[1][:, part], preferred_element_type=f32)
         y = y.astype(bf16)
-        top = 0
-        for ref in outs[i]:
-            ref[...] = y[top : top + ref.shape[0]]
-            top += ref.shape[0]
-
-
-def mlp(mine, blocks, weights, cut=1, begun=None, lits=()):
+        if i < 3 or len(outs) == 4:
+            outs[i][...] = y
+        else:
+            outs[3][...] = y[: rows // 2]
+            outs[4][...] = y[rows // 2 :]
+
+
+def mlp(mine, blocks, weights, begun=None, lits=(), halve=False):
     spec = [(len(arrays), spans, gain, i) for arrays, spans, gain, i in blocks]
     rows, quarter = sum(n for _, _, n in blocks[0][1]), blocks[0][0][0].shape[1]
     flat = [*(begun or ()), *[a for arrays, *_ in blocks for a in arrays], *[a for a, _, _ in lits]]
     hidden = weights[0].shape[1]
     flops = 2 * rows * quarter * len(blocks) * hidden * 4
     if lits:
-        out = [pltpu.VMEM((rows // cut, quarter), bf16)] * cut + [pltpu.VMEM((rows, quarter), bf16)] * 3
+        out = [pltpu.VMEM((rows, quarter), bf16)] * 3
+        out += [pltpu.VMEM((rows // 2, quarter), bf16)] * 2 if halve else out[:1]
         flops += 2 * rows * quarter * 4 * hidden * 2
     else:
         out = [pltpu.VMEM((rows, 2 * hidden), f32)] * 2 + [pltpu.VMEM((rows, HD), f32)]
         weights = weights[:4]
     weights = [pltpu.with_memory_space_constraint(w, pltpu.VMEM) for w in weights]
-    out = kernel(
-        functools.partial(mlp_body, spec, [(row, n) for _, row, n in lits], cut, begun is not None),
+    return kernel(
+        functools.partial(mlp_body, spec, [(row, n) for _, row, n in lits], begun is not None),
         out,
         [SMEM] + [VMEM] * (len(flat) + len(weights)),
         [VMEM] * len(out),
         12,
         cost=pl.CostEstimate(flops=flops, bytes_accessed=8 << 20, transcendentals=0),
     )(mine, *flat, *weights)
-    return (out[:cut], *out[cut:]) if lits else out
 
 
 def add(*parts):
@@ -275,6 +271,22 @@
     for part in parts[1:]:
         total = total + part.astype(f32)
     return total.astype(bf16)
+
+
+def sum_body(tops, *refs):
+    out_ref = refs[-1]
+    rows = out_ref.shape[0]
+    total = refs[0][tops[0] : tops[0] + rows].astype(f32)
+    for ref, top in zip(refs[1:-1], tops[1:]):
+        total += ref[top : top + rows].astype(f32)
+    out_ref[...] = total.astype(bf16)
+
+
+def sum_rows(rows, *parts):
+    shape = (rows, parts[0][0].shape[1])
+    return kernel(
+        functools.partial(sum_body, [top for _, top in parts]), pltpu.VMEM(shape, bf16), [VMEM] * len(parts), VMEM, 4
+    )(*[a for a, _ in parts])
 
 
 def final_body(shape, stream_ref, taken_ref, *refs):
@@ -283,11 +295,11 @@
     total = stream_ref[...].astype(f32)
     at = 0
     for n in shape:
-        part = refs.pop(0)[...].astype(f32)
+        part = refs.pop(0)[...]
         for _ in range(n - 1):
-            part += refs.pop(0)[...].astype(f32)
+            part = (part.astype(f32) + refs.pop(0)[...].astype(f32)).astype(bf16)
         rows = part.shape[0]
-        total += jnp.dot(taken_ref[:, at : at + rows], part.astype(bf16), preferred_element_type=f32)
+        total += jnp.dot(taken_ref[:, at : at + rows], part, preferred_element_type=f32)
         at += rows
     out_ref[0] = total.astype(bf16)
 
@@ -307,7 +319,7 @@
     shard, quarter = query_proj.shape[1:]
     seq, experts = lax.axis_size("seq"), lax.axis_size("exp")
     sid = lax.axis_index("seq").astype(jnp.int32)[None]
-    eid = lax.axis_index("exp").astype(jnp.int32)[None]
+    eid = lax.axis_index("exp").astype(jnp.int32)[None] ^ (sid & 1)
     fid = lax.axis_index("ff").astype(jnp.int32)[None]
     cap = max(2, 3 * shard // (2 * experts))
     slots = experts * cap
@@ -324,6 +336,7 @@
     )(far_off(key_proj), far_off(value_proj))
     kv2 = flip(kv, later=True, seq=2)
     kv1 = flip(kv, later=True, seq=1)
+    kv3 = flip(kv2, seq=1)
     extras = 2 if two else 1
     query, res, taken, *extra, lit = kernel(
         functools.partial(prep_body, experts, cap),
@@ -339,70 +352,76 @@
         8,
         scratch=[near((1, shard), jnp.int32), near((1, shard), f32), near((quarter,), f32), dma((5,))],
     )(eid, far_off(query_proj), far_off(residual), far_off(expert_ids[0, :, 0][None]), far_off(router_logit), far_off(norm_gain))
-    kv3 = flip(kv2, seq=1)
-
-    layout = [(0, cap, 0), (cap, cap, 1), (cap, cap, None)] if two else [(0, slots, None)]
+
+    layout = [(0, cap, True), (cap, cap, False)] if two else [(0, slots, False)]
+    if two:
+        extra[1] = flip(extra[1], seq=1)
     stream, *send = kernel(
         functools.partial(attend_body, HEADS // KVH, seq, extras, layout),
-        [near((shard, quarter), bf16)] + [near((n + (0 if e is None else EXTRA), quarter), bf16) for _, n, e in layout],
+        [near((shard, quarter), bf16)] + [near((n + (EXTRA if e else 0), quarter), bf16) for _, n, e in layout],
         [SMEM] + [VMEM] * (3 + seq + extras),
         (VMEM,) * (1 + len(layout)),
         8,
     )(sid, query, res, taken, kv, kv1, kv2, kv3, *extra)
 
-    weights = (gate_weight[0], up_weight[0], down_weight[0])
-    tied, send = lax.optimization_barrier((weights, send))
+    rows = 2 * cap if two else slots
     if two:
-        mine, other, bare = send
-        sel = join(flip(mine, ff=3), flip(bare, exp=1, ff=3))
-        non = join(flip(mine, ff=1), flip(bare, exp=1, ff=1))
-        own = [mine, flip(other, exp=1)]
-        own_x = [flip(mine, seq=2), flip(other, seq=2, exp=1)]
-        far_x = [flip(own_x[0], ff=2), flip(own_x[1], ff=2)]
-        one = ((0, 0, cap), (0, cap + EXTRA, cap)), cap
-        both = ((0, 0, cap), (1, 0, cap)), cap
-        lit_of = ((cap + 3, cap), (cap + 3, cap))
-        cut = 2
+        got = flip(send[1], seq=1)
+        halves = [send[0], got]
+        block = kernel(join_body, near((rows + EXTRA, quarter), bf16), [VMEM] * 2, VMEM, 4)(*halves)
+        lit_of = ((rows + 3, cap), (rows + 6, cap))
+        spans, gain_row = ((0, 0, cap), (1, 0, cap)), cap
     else:
         block = lax.all_to_all(send[0], "exp", split_axis=0, concat_axis=0, tiled=True)
         lit = lax.all_to_all(lit[0], "exp", split_axis=0, concat_axis=0, tiled=True)
         lit = jnp.pad(jnp.stack(split(lit)), ((0, 0), (0, quarter - slots)))
-        tail = jnp.concatenate([extra[0][:3], lit, extra[0][6:]], axis=0)
-        block = jnp.concatenate([block, tail], axis=0)
-        own, own_x = [block], [flip(block, seq=2)]
-        sel, non = flip(block, ff=3), flip(block, ff=1)
-        one = both = ((0, 0, slots),), slots
-        far_x = [flip(own_x[0], ff=2)]
-        lit_of = ((slots + 3, slots),)
-        cut = 1
-    partner = [flip(w, seq=1) for w in tied]
-    pairs = [w for each in zip(load(weights), load(partner)) for w in each]
-    far = flip(sel, ff=1)
-    sel_x = flip(sel, seq=2)
+        block = jnp.concatenate([block, extra[0][:3], lit, extra[0][6:]], axis=0)
+        halves = [block]
+        lit_of = ((rows + 3, slots),)
+        spans, gain_row = ((0, 0, rows),), rows
+
+    def each(arrays, *args, **bits):
+        return [flip(a, *args, **bits) for a in arrays]
+
+    weights = (gate_weight[0], up_weight[0], down_weight[0])
+    sel = each(halves, two, ff=2)
+    non = flip(block, two, ff=1)
+    own_x = flip(block, two, seq=2)
+    own = flip(block, two) if two else block
+    partner = each(weights, seq=1)
+    pairs = [w for both in zip(load(weights), load(partner)) for w in both]
+    far = each(sel, ff=1)
+    sel_x = each(sel, seq=2)
     non_x = flip(non, seq=2)
-
-    def lit_in(arrays):
-        return [(a, row, n) for a, (row, n) in zip(arrays, lit_of)]
-
-    begun = mlp(fid, [(own, *both, 0), ([sel], *one, 3), ([non], *one, 1)], pairs)
-    p0, p1, p2, p3 = mlp(fid, [([far], *one, 2)], pairs, cut, begun, lit_in(own))
-    begun = mlp(fid, [(own_x, *both, 0), (far_x, *both, 2), ([sel_x], *one, 3)], pairs)
-    o0, o1, o2, o3 = mlp(fid, [([non_x], *one, 1)], pairs, cut, begun, lit_in(own_x))
-
-    back_x = flip(o2, ff=1)
-    back = flip(p2, ff=1)
-    tot_non = add(p1, flip(o1, seq=2))
-    tot_sel = add(p3, back, flip(add(o3, back_x), seq=2))
+    far_x = each(sel_x, ff=1)
+
+    def blocks(*parts):
+        return [([a], ((0, 0, rows),), rows, i) if not isinstance(a, list) else (a, spans, gain_row, i) for a, i in parts]
+
+    def lit_in(array):
+        return [(array, row, n) for row, n in lit_of]
+
+    begun = mlp(fid, blocks((own, 0), (sel, 2), (non, 1)), pairs)
+    p0, p1, p2, p3 = mlp(fid, blocks((far, 3)), pairs, begun, lit_in(own))
+    begun = mlp(fid, blocks((own_x, 0), (sel_x, 2), (non_x, 1)), pairs)
+    o0, o1, o2, *o3 = mlp(fid, blocks((far_x, 3)), pairs, begun, lit_in(own_x), two)
+
+    part = cap if two else slots
+    order = range(len(o3))
+    back_x = each(o3, ff=1)
+    back = flip(p3, ff=1)
+    over = each([sum_rows(part, (o2, i * part), (back_x[i], 0)) for i in order], seq=2)
+    last = [sum_rows(part, (p2, i * part), (back, i * part), (over[i], 0)) for i in order]
+    last = each(last, two, ff=2)
+    tot_non = sum_rows(rows, (p1, 0), (flip(o1, seq=2), 0))
+    home = flip(p0, two) if two else p0
+    most = [home, flip(o0, two, seq=2), flip(tot_non, two, ff=1)]
+    most = [sum_rows(part, *[(a, i * part) for a in most]) for i in order]
     if two:
-        parts = [
-            p0[0], flip(o0[0], seq=2), flip(tot_non[:cap], ff=1), flip(tot_sel[:cap], ff=3),
-            flip(p0[1], exp=1), flip(o0[1], seq=2, exp=1),
-            flip(tot_non[cap:], exp=1, ff=1), flip(tot_sel[cap:], exp=1, ff=3),
-        ]
-        shape = (4, 4)
+        parts = [most[0], last[0], flip(most[1], seq=1), flip(last[1], seq=1)]
+        shape = (2, 2)
     else:
-        parts = add(p0[0], flip(o0[0], seq=2), flip(tot_non, ff=1), flip(tot_sel, ff=3))
-        parts = [lax.all_to_all(parts, "exp", split_axis=0, concat_axis=0, tiled=True)]
+        parts = [lax.all_to_all(add(most[0], last[0]), "exp", split_axis=0, concat_axis=0, tiled=True)]
         shape = (1,)
     return kernel(
         functools.partial(final_body, shape), like((1, shard, quarter), bf16), [VMEM] * (2 + len(parts)), VMEM, 8

time: 88.7 us -> 87.8 us (0.990)
  starting transfers between devices: 48.3 us -> 36.1 us
  waiting for transfers between devices: 21 us -> 32.3 us
  Pallas kernels: 16.9 us -> 17.8 us
    ppermute x29 -> x33, starting transfers between devices: 48.3 us -> 36.1 us  [flip(): return lax.ppermute(value, axes, pairs)]
    ppermute x29 -> x33, waiting for transfers between devices: 21 us -> 32.3 us  [flip(): return lax.ppermute(value, axes, pairs)]
    pallas_call x2 -> x8, Pallas kernels: 0.04 us -> 1.08 us  [the longest x1 0.74 us: body(): kernel(join_body, near((rows + EXTRA, quarter), bf16), [VMEM] * 2, VMEM, 4)]
  transfers between devices with their start and end apart: 29 -> 33, of which waited for: 9 -> 13; matrix products, arithmetic and copies ran while one was open for 0% -> 0% of each run, Pallas kernels for 15% -> 19%
where the time goes in v2:
time: 87.8 us; the launch traced here: 87.5 us
  starting transfers between devices  36.1 us (41%)
  waiting for transfers between devices  32.3 us (37%)
  Pallas kernels  17.8 us (20%)
  local copies, waits for them, and re-layouts  1.09 us (1%)
    ppermute x33, starting transfers between devices, flip(): return lax.ppermute(value, axes, pairs)  36.1 us
    ppermute x33, waiting for transfers between devices, flip(): return lax.ppermute(value, axes, pairs)  32.3 us
    pallas_call x4, Pallas kernels, mlp(): kernel(functools.partial(mlp_body, spec, [(row, n) for _, row, n in lits]...  6.96 us
    pallas_call x2, Pallas kernels, load(): kernel(load_body, [pltpu.VMEM(a.shape, a.dtype) for a in arrays], [RAW] *...  4.3 us
    pallas_call x1, Pallas kernels, body(): kernel(functools.partial(attend_body, HEADS // KVH, seq, extras, layout),...  1.91 us
    pallas_call x1, Pallas kernels, body(): kernel(functools.partial(prep_body, experts, cap), (near((shard, quarter)...  1.79 us
  transfers between devices with their start and end apart: 33, of which 13 were waited for; matrix products, arithmetic and copies ran while one was open for 0% of the time, Pallas kernels for 19%

profile of v2, /device:TPU:0, one launch (start us, length us, event | category | flops | bytes accessed | tf_op | source)
XLA Modules:
  0.0 87.5 jit_solution(14345009756001018475)
XLA Ops:
  1.8 4.4 %collective-permute-start.1 = (bf16[256,128]{1,0:T(8,128)(2,1)S(1)}, bf16[256,128]{1,0:T(8,128)(2,1)S(1)}, u32[]{:S(2)}, u32[]{:S(2)}) collective-permute-start(bf16[256,128]{1,0:T(8,128)(2,1)S(1)} %shard_map.101.refs_0_), channel_id=1, source_target_pairs={{0,16},{1,17},{2,18},{3,19},{4,20},{5,21},{6,22},{7,23},{8,24},{9,... | collective-permute-start | bytes 196616 | tf_op jit(solution)/shard_map/ppermute | solution.py:49
  6.2 1.8 %shard_map.100 = (bf16[128,640]{1,0:T(8,128)(2,1)S(1)}, bf16[128,640]{1,0:T(8,128)(2,1)S(1)}, bf16[128,192]{1,0:T(8,128)(2,1)S(1)}, bf16[16,640]{1,0:T(8,128)(2,...) custom-call(s32[1]{0:T(128)S(6)} %xor.3.where_ref, bf16[1,128,640]{2,1,0:T(8,128)(2,1)} %q_in.1, ...), custom_call_target="tpu_custom_call" | custom-call | tf_op jit(solution)/shard_map/pallas_call | solution.py:341
  9.3 2.1 %collective-permute-start = (bf16[256,128]{1,0:T(8,128)(2,1)S(1)}, bf16[256,128]{1,0:T(8,128)(2,1)S(1)}, u32[]{:S(2)}, u32[]{:S(2)}) collective-permute-start(bf16[256,128]{1,0:T(8,128)(2,1)S(1)} %shard_map.101.refs_0_), channel_id=1, source_target_pairs={{0,8},{1,9},{2,10},{3,11},{4,12},{5,13},{6,14},{7,15},{16,24},{17,... | collective-permute-start | bytes 196616 | tf_op jit(solution)/shard_map/ppermute | solution.py:49
  12.7 1.9 %shard_map.102 = (bf16[128,640]{1,0:T(8,128)(2,1)S(1)}, bf16[112,640]{1,0:T(8,128)(2,1)S(1)}, bf16[96,640]{1,0:T(8,128)(2,1)S(1)}) custom-call(s32[1]{0:T(128)} %bitcast.where_ref, bf16[128,640]{1,0:T(8,128)(2,1)S(1)} %get-tuple-element.34.q_ref, bf16[128,640]{1,0:T(8,128)(2,1)S(1)} %get-tuple-element.35.res_ref, ...), custom_call_target="tpu_custom_call" | custom-call | tf_op jit(solution)/shard_map/pallas_call | solution.py:359
  14.9 2.6 %collective-permute-start.6 = (bf16[112,640]{1,0:T(8,128)(2,1)S(1)}, bf16[112,640]{1,0:T(8,128)(2,1)S(1)}, u32[]{:S(2)}, u32[]{:S(2)}) collective-permute-start(bf16[112,640]{1,0:T(8,128)(2,1)S(1)} %get-tuple-element.40.keep_ref), channel_id=1, source_target_pairs={{0,2},{1,3},{2,0},{3,1},{4,6},{5,7},{6,4},{7,5},{8,14},{9,15},{10,... | collective-permute-start | bytes 430088 | tf_op jit(solution)/shard_map/ppermute | solution.py:49
  18.6 9.1 %collective-permute-done.6.refs_1_ = bf16[112,640]{1,0:T(8,128)(2,1)S(1)} collective-permute-done((bf16[112,640]{1,0:T(8,128)(2,1)S(1)}, bf16[112,640]{1,0:T(8,128)(2,1)S(1)}, u32[]{:S(2)}, u32[]{:S(2)}) %collective-permute-start.6) | collective-permute-done | bytes 143392 | tf_op jit(solution)/shard_map/ppermute | solution.py:49
  31.4 1.9 %collective-permute-done.16.refs_1_ = bf16[112,640]{1,0:T(8,128)(2,1)} collective-permute-done((bf16[112,640]{1,0:T(8,128)(2,1)S(1)}, bf16[112,640]{1,0:T(8,128)(2,1)}, u32[]{:S(2)}, u32[]{:S(2)}) %collective-permute-start.16) | collective-permute-done | bytes 143392 | tf_op jit(solution)/shard_map/ppermute | solution.py:49
  34.1 4.2 %collective-permute-done.17.refs_2_ = bf16[96,640]{1,0:T(8,128)(2,1)} collective-permute-done((bf16[96,640]{1,0:T(8,128)(2,1)S(1)}, bf16[96,640]{1,0:T(8,128)(2,1)}, u32[]{:S(2)}, u32[]{:S(2)}) %collective-permute-start.17) | collective-permute-done | bytes 122912 | tf_op jit(solution)/shard_map/ppermute | solution.py:49
  40.5 1.6 %collective-permute-start.5 = (bf16[208,640]{1,0:T(8,128)(2,1)}, bf16[208,640]{1,0:T(8,128)(2,1)S(1)}, u32[]{:S(2)}, u32[]{:S(2)}) collective-permute-start(bf16[208,640]{1,0:T(8,128)(2,1)} %shard_map.103), channel_id=1, source_target_pairs={{0,0},{1,1},{2,2},{3,3},{4,4},{5,5},{6,6},{7,7},{8,12},{9,13},{10,... | collective-permute-start | bytes 798728 | tf_op jit(solution)/shard_map/ppermute | solution.py:49
  44.3 2.1 %shard_map.104 = (bf16[2560,256]{1,0:T(8,128)(2,1)S(1)}, bf16[2560,256]{1,0:T(8,128)(2,1)S(1)}, bf16[256,2560]{1,0:T(8,128)(2,1)S(1)}) custom-call(bf16[2560,256]{1,0:T(8,128)(2,1)} %bitcast.8, bf16[2560,256]{1,0:T(8,128)(2,1)} %bitcast.10, bf16[256,2560]{1,0:T(8,128)(2,1)} %bitcast.12), custom_call_target="tpu_custom_call" | custom-call | tf_op jit(solution)/shard_map/pallas_call | solution.py:176
  47.5 2.2 %shard_map.105 = (bf16[2560,256]{1,0:T(8,128)(2,1)S(1)}, bf16[2560,256]{1,0:T(8,128)(2,1)S(1)}, bf16[256,2560]{1,0:T(8,128)(2,1)S(1)}) custom-call(bf16[2560,256]{1,0:T(8,128)(2,1)} %collective-permute-done.9.refs_0_, bf16[2560,256]{1,0:T(8,128)(2,1)} %copy-done.8, bf16[256,2560]{1,0:T(8,128)(2,1)} %collective-permute-done.11.refs_2_), custom_call_target="tpu_custom_call" | custom-call | tf_op jit(solution)/shard_map/pallas_call | solution.py:176
  50.9 1.6 %collective-permute-done.18.refs_3_ = bf16[208,640]{1,0:T(8,128)(2,1)} collective-permute-done((bf16[208,640]{1,0:T(8,128)(2,1)S(1)}, bf16[208,640]{1,0:T(8,128)(2,1)}, u32[]{:S(2)}, u32[]{:S(2)}) %collective-permute-start.18) | collective-permute-done | bytes 266272 | tf_op jit(solution)/shard_map/ppermute | solution.py:49
  52.5 2.3 %shard_map.108 = (f32[192,512]{1,0:T(8,128)S(1)}, f32[192,512]{1,0:T(8,128)S(1)}, f32[192,128]{1,0:T(8,128)S(1)}) custom-call(s32[1]{0:T(128)} %bitcast.3.where_ref, bf16[208,640]{1,0:T(8,128)(2,1)S(1)} %collective-permute-done.15.refs_0_.refs_5_.refs_6_, bf16[112,640]{1,0:T(8,128)(2,1)} %collective-permute-done.16.refs_1_, ...), custom_call_target="tpu_custom_call" | custom-call | flops 754974720 | bytes 8388608 | tf_op jit(solution)/shard_map/pallas_call | solution.py:259
  54.8 2.3 %shard_map.109 = (bf16[192,640]{1,0:T(8,128)(2,1)S(1)}, bf16[192,640]{1,0:T(8,128)(2,1)S(1)}, bf16[192,640]{1,0:T(8,128)(2,1)S(1)}, bf16[96,640]{1,0:T(8,128)(2,1)S(1)}, bf16[96,640]{1,0:T(8,128)(2,1)S(1)}) custom-call(s32[1]{0:T(128)} %bitcast.3.where_ref, f32[192,512]{1,0:T(8,128)S(1)} %get-tuple-element.52.refs_0_, ...), custom_call_target="tpu_custom_call" | custom-call | flops 754974720 | bytes 8388608 | tf_op jit(solution)/shard_map/pallas_call | solution.py:259
  57.1 2.1 %collective-permute-start.29 = (bf16[96,640]{1,0:T(8,128)(2,1)S(1)}, bf16[96,640]{1,0:T(8,128)(2,1)S(1)}, u32[]{:S(2)}, u32[]{:S(2)}) collective-permute-start(bf16[96,640]{1,0:T(8,128)(2,1)S(1)} %get-tuple-element.62), channel_id=1, source_target_pairs={{0,1},{1,0},{2,3},{3,2},{4,5},{5,4},{6,7},{7,6},{8,9},{9,8},{10,11... | collective-permute-start | bytes 368648 | tf_op jit(solution)/shard_map/ppermute | solution.py:49
  61.1 1.3 %shard_map.107 = (bf16[192,640]{1,0:T(8,128)(2,1)S(1)}, bf16[192,640]{1,0:T(8,128)(2,1)S(1)}, bf16[192,640]{1,0:T(8,128)(2,1)S(1)}, bf16[192,640]{1,0:T(8,128)(2,1)S(1)}) custom-call(s32[1]{0:T(128)} %bitcast.3.where_ref, f32[192,512]{1,0:T(8,128)S(1)} %get-tuple-element.46.refs_0_, f32[192,512]{1,0:T(8,128)S(1)} %get-tuple-element.47.refs_1_, ...), custom_call_target="tpu_custom_call" | custom-call | flops 754974720 | bytes 8388608 | tf_op jit(solution)/shard_map/pallas_call | solution.py:259
  62.6 2.0 %collective-permute-start.25 = (bf16[96,640]{1,0:T(8,128)(2,1)S(1)}, bf16[96,640]{1,0:T(8,128)(2,1)S(1)}, u32[]{:S(2)}, u32[]{:S(2)}) collective-permute-start(bf16[96,640]{1,0:T(8,128)(2,1)S(1)} %get-tuple-element.61), channel_id=1, source_target_pairs={{0,1},{1,0},{2,3},{3,2},{4,5},{5,4},{6,7},{7,6},{8,9},{9,8},{10,11... | collective-permute-start | bytes 368648 | tf_op jit(solution)/shard_map/ppermute | solution.py:49
  64.6 1.3 %collective-permute-start.30 = (bf16[96,640]{1,0:T(8,128)(2,1)S(1)}, bf16[96,640]{1,0:T(8,128)(2,1)S(1)}, u32[]{:S(2)}, u32[]{:S(2)}) collective-permute-start(bf16[96,640]{1,0:T(8,128)(2,1)S(1)} %shard_map.115), channel_id=1, source_target_pairs={{0,16},{1,17},{2,18},{3,19},{4,20},{5,21},{6,22},{7,23},{8,24},{9,... | collective-permute-start | bytes 368648 | tf_op jit(solution)/shard_map/ppermute | solution.py:49
  67.4 3.8 %collective-permute-done.25.refs_1_ = bf16[96,640]{1,0:T(8,128)(2,1)S(1)} collective-permute-done((bf16[96,640]{1,0:T(8,128)(2,1)S(1)}, bf16[96,640]{1,0:T(8,128)(2,1)S(1)}, u32[]{:S(2)}, u32[]{:S(2)}) %collective-permute-start.25) | collective-permute-done | bytes 122912 | tf_op jit(solution)/shard_map/ppermute | solution.py:49
  71.2 1.3 %collective-permute-start.23 = (bf16[192,640]{1,0:T(8,128)(2,1)S(1)}, bf16[192,640]{1,0:T(8,128)(2,1)S(1)}, u32[]{:S(2)}, u32[]{:S(2)}) collective-permute-start(bf16[192,640]{1,0:T(8,128)(2,1)S(1)} %shard_map.110), channel_id=1, source_target_pairs={{0,1},{1,0},{2,3},{3,2},{4,5},{5,4},{6,7},{7,6},{8,13},{9,12},{10,... | collective-permute-start | bytes 737288 | tf_op jit(solution)/shard_map/ppermute | solution.py:49
  73.5 2.7 %collective-permute-start.31 = (bf16[96,640]{1,0:T(8,128)(2,1)S(1)}, bf16[96,640]{1,0:T(8,128)(2,1)S(1)}, u32[]{:S(2)}, u32[]{:S(2)}) collective-permute-start(bf16[96,640]{1,0:T(8,128)(2,1)S(1)} %shard_map.116), channel_id=1, source_target_pairs={{0,2},{1,3},{2,0},{3,1},{4,6},{5,7},{6,4},{7,5},{8,14},{9,15},{10,... | collective-permute-start | bytes 368648 | tf_op jit(solution)/shard_map/ppermute | solution.py:49
  77.6 2.2 %collective-permute-start.27 = (bf16[96,640]{1,0:T(8,128)(2,1)S(1)}, bf16[96,640]{1,0:T(8,128)(2,1)S(1)}, u32[]{:S(2)}, u32[]{:S(2)}) collective-permute-start(bf16[96,640]{1,0:T(8,128)(2,1)S(1)} %shard_map.113), channel_id=1, source_target_pairs={{0,2},{1,3},{2,0},{3,1},{4,6},{5,7},{6,4},{7,5},{8,14},{9,15},{10,... | collective-permute-start | bytes 368648 | tf_op jit(solution)/shard_map/ppermute | solution.py:49
  79.7 2.5 %collective-permute-done.31 = bf16[96,640]{1,0:T(8,128)(2,1)S(1)} collective-permute-done((bf16[96,640]{1,0:T(8,128)(2,1)S(1)}, bf16[96,640]{1,0:T(8,128)(2,1)S(1)}, u32[]{:S(2)}, u32[]{:S(2)}) %collective-permute-start.31) | collective-permute-done | bytes 122912 | tf_op jit(solution)/shard_map/ppermute | solution.py:49
  83.0 3.6 %collective-permute-done.27.refs_1_ = bf16[96,640]{1,0:T(8,128)(2,1)S(1)} collective-permute-done((bf16[96,640]{1,0:T(8,128)(2,1)S(1)}, bf16[96,640]{1,0:T(8,128)(2,1)S(1)}, u32[]{:S(2)}, u32[]{:S(2)}) %collective-permute-start.27) | collective-permute-done | bytes 122912 | tf_op jit(solution)/shard_map/ppermute | solution.py:49
  (78 shorter events, 24.2 us)
Async XLA Ops:
  0.0 40.5 %collective-permute-start.10 = (bf16[2560,256]{1,0:T(8,128)(2,1)}, bf16[2560,256]{1,0:T(8,128)(2,1)S(1)}, u32[]{:S(2)}, u32[]{:S(2)}) collective-permute-start(bf16[2560,256]{1,0:T(8,128)(2,1)} %bitcast.9), channel_id=1, source_target_pairs={{0,8},{1,9},{2,10},{3,11},{4,12},{5,13},{6,14},{7,15},{8,0},{9,1},... | collective-permute-start | bytes 3932168 | tf_op jit(solution)/shard_map/ppermute | solution.py:49
  0.5 41.7 %collective-permute-start.11 = (bf16[256,2560]{1,0:T(8,128)(2,1)}, bf16[256,2560]{1,0:T(8,128)(2,1)}, u32[]{:S(2)}, u32[]{:S(2)}) collective-permute-start(bf16[256,2560]{1,0:T(8,128)(2,1)} %bitcast.11), channel_id=1, source_target_pairs={{0,8},{1,9},{2,10},{3,11},{4,12},{5,13},{6,14},{7,15},{8,0},{9,1},... | collective-permute-start | bytes 3932168 | tf_op jit(solution)/shard_map/ppermute | solution.py:49
  0.5 42.8 %collective-permute-start.9 = (bf16[2560,256]{1,0:T(8,128)(2,1)}, bf16[2560,256]{1,0:T(8,128)(2,1)}, u32[]{:S(2)}, u32[]{:S(2)}) collective-permute-start(bf16[2560,256]{1,0:T(8,128)(2,1)} %bitcast.7), channel_id=1, source_target_pairs={{0,8},{1,9},{2,10},{3,11},{4,12},{5,13},{6,14},{7,15},{8,0},{9,1},... | collective-permute-start | bytes 3932168 | tf_op jit(solution)/shard_map/ppermute | solution.py:49
  1.8 9.6 %collective-permute-start.1 = (bf16[256,128]{1,0:T(8,128)(2,1)S(1)}, bf16[256,128]{1,0:T(8,128)(2,1)S(1)}, u32[]{:S(2)}, u32[]{:S(2)}) collective-permute-start(bf16[256,128]{1,0:T(8,128)(2,1)S(1)} %shard_map.101.refs_0_), channel_id=1, source_target_pairs={{0,16},{1,17},{2,18},{3,19},{4,20},{5,21},{6,22},{7,23},{8,24},{9,... | collective-permute-start | bytes 196616 | tf_op jit(solution)/shard_map/ppermute | solution.py:49
  14.9 12.9 %collective-permute-start.6 = (bf16[112,640]{1,0:T(8,128)(2,1)S(1)}, bf16[112,640]{1,0:T(8,128)(2,1)S(1)}, u32[]{:S(2)}, u32[]{:S(2)}) collective-permute-start(bf16[112,640]{1,0:T(8,128)(2,1)S(1)} %get-tuple-element.40.keep_ref), channel_id=1, source_target_pairs={{0,2},{1,3},{2,0},{3,1},{4,6},{5,7},{6,4},{7,5},{8,14},{9,15},{10,... | collective-permute-start | bytes 430088 | tf_op jit(solution)/shard_map/ppermute | solution.py:49
  17.5 12.9 %collective-permute-start.7 = (bf16[96,640]{1,0:T(8,128)(2,1)S(1)}, bf16[96,640]{1,0:T(8,128)(2,1)S(1)}, u32[]{:S(2)}, u32[]{:S(2)}) collective-permute-start(bf16[96,640]{1,0:T(8,128)(2,1)S(1)} %collective-permute-done.4.got_ref), channel_id=1, source_target_pairs={{0,2},{1,3},{2,0},{3,1},{4,6},{5,7},{6,4},{7,5},{8,14},{9,15},{10,... | collective-permute-start | bytes 368648 | tf_op jit(solution)/shard_map/ppermute | solution.py:49
  30.4 9.4 %collective-permute-start.8 = (bf16[208,640]{1,0:T(8,128)(2,1)}, bf16[208,640]{1,0:T(8,128)(2,1)S(1)}, u32[]{:S(2)}, u32[]{:S(2)}) collective-permute-start(bf16[208,640]{1,0:T(8,128)(2,1)} %shard_map.103), channel_id=1, source_target_pairs={{0,1},{1,0},{2,3},{3,2},{4,5},{5,4},{6,7},{7,6},{8,13},{9,12},{10,... | collective-permute-start | bytes 798728 | tf_op jit(solution)/shard_map/ppermute | solution.py:49
  38.3 11.4 %collective-permute-start.15 = (bf16[208,640]{1,0:T(8,128)(2,1)}, bf16[208,640]{1,0:T(8,128)(2,1)S(1)}, u32[]{:S(2)}, u32[]{:S(2)}) collective-permute-start(bf16[208,640]{1,0:T(8,128)(2,1)} %shard_map.103), channel_id=1, source_target_pairs={{0,16},{1,17},{2,18},{3,19},{4,20},{5,21},{6,22},{7,23},{8,28},{9,... | collective-permute-start | bytes 798728 | tf_op jit(solution)/shard_map/ppermute | solution.py:49
  39.8 12.7 %collective-permute-start.18 = (bf16[208,640]{1,0:T(8,128)(2,1)S(1)}, bf16[208,640]{1,0:T(8,128)(2,1)}, u32[]{:S(2)}, u32[]{:S(2)}) collective-permute-start(bf16[208,640]{1,0:T(8,128)(2,1)S(1)} %collective-permute-done.8.refs_3_), channel_id=1, source_target_pairs={{0,16},{1,17},{2,18},{3,19},{4,20},{5,21},{6,22},{7,23},{8,24},{9,... | collective-permute-start | bytes 798728 | tf_op jit(solution)/shard_map/ppermute | solution.py:49
  40.5 19.4 %collective-permute-start.5 = (bf16[208,640]{1,0:T(8,128)(2,1)}, bf16[208,640]{1,0:T(8,128)(2,1)S(1)}, u32[]{:S(2)}, u32[]{:S(2)}) collective-permute-start(bf16[208,640]{1,0:T(8,128)(2,1)} %shard_map.103), channel_id=1, source_target_pairs={{0,0},{1,1},{2,2},{3,3},{4,4},{5,5},{6,6},{7,7},{8,12},{9,13},{10,... | collective-permute-start | bytes 798728 | tf_op jit(solution)/shard_map/ppermute | solution.py:49
  42.2 12.7 %collective-permute-start.19 = (bf16[112,640]{1,0:T(8,128)(2,1)}, bf16[112,640]{1,0:T(8,128)(2,1)}, u32[]{:S(2)}, u32[]{:S(2)}) collective-permute-start(bf16[112,640]{1,0:T(8,128)(2,1)} %collective-permute-done.16.refs_1_), channel_id=1, source_target_pairs={{0,1},{1,0},{2,3},{3,2},{4,5},{5,4},{6,7},{7,6},{8,9},{9,8},{10,11... | collective-permute-start | bytes 430088 | tf_op jit(solution)/shard_map/ppermute | solution.py:49
  43.4 11.5 %collective-permute-start.20 = (bf16[96,640]{1,0:T(8,128)(2,1)}, bf16[96,640]{1,0:T(8,128)(2,1)}, u32[]{:S(2)}, u32[]{:S(2)}) collective-permute-start(bf16[96,640]{1,0:T(8,128)(2,1)} %collective-permute-done.17.refs_2_), channel_id=1, source_target_pairs={{0,1},{1,0},{2,3},{3,2},{4,5},{5,4},{6,7},{7,6},{8,9},{9,8},{10,11... | collective-permute-start | bytes 368648 | tf_op jit(solution)/shard_map/ppermute | solution.py:49
  49.7 11.4 %collective-permute-start.12 = (bf16[112,640]{1,0:T(8,128)(2,1)S(1)}, bf16[112,640]{1,0:T(8,128)(2,1)S(1)}, u32[]{:S(2)}, u32[]{:S(2)}) collective-permute-start(bf16[112,640]{1,0:T(8,128)(2,1)S(1)} %copy-done.5), channel_id=1, source_target_pairs={{0,1},{1,0},{2,3},{3,2},{4,5},{5,4},{6,7},{7,6},{8,9},{9,8},{10,11... | collective-permute-start | bytes 430088 | tf_op jit(solution)/shard_map/ppermute | solution.py:49
  52.5 8.6 %collective-permute-start.13 = (bf16[96,640]{1,0:T(8,128)(2,1)S(1)}, bf16[96,640]{1,0:T(8,128)(2,1)S(1)}, u32[]{:S(2)}, u32[]{:S(2)}) collective-permute-start(bf16[96,640]{1,0:T(8,128)(2,1)S(1)} %copy-done.7), channel_id=1, source_target_pairs={{0,1},{1,0},{2,3},{3,2},{4,5},{5,4},{6,7},{7,6},{8,9},{9,8},{10,11... | collective-permute-start | bytes 368648 | tf_op jit(solution)/shard_map/ppermute | solution.py:49
  57.1 7.4 %collective-permute-start.29 = (bf16[96,640]{1,0:T(8,128)(2,1)S(1)}, bf16[96,640]{1,0:T(8,128)(2,1)S(1)}, u32[]{:S(2)}, u32[]{:S(2)}) collective-permute-start(bf16[96,640]{1,0:T(8,128)(2,1)S(1)} %get-tuple-element.62), channel_id=1, source_target_pairs={{0,1},{1,0},{2,3},{3,2},{4,5},{5,4},{6,7},{7,6},{8,9},{9,8},{10,11... | collective-permute-start | bytes 368648 | tf_op jit(solution)/shard_map/ppermute | solution.py:49
  59.2 7.4 %collective-permute-start.22 = (bf16[192,640]{1,0:T(8,128)(2,1)S(1)}, bf16[192,640]{1,0:T(8,128)(2,1)S(1)}, u32[]{:S(2)}, u32[]{:S(2)}) collective-permute-start(bf16[192,640]{1,0:T(8,128)(2,1)S(1)} %get-tuple-element.57), channel_id=1, source_target_pairs={{0,16},{1,17},{2,18},{3,19},{4,20},{5,21},{6,22},{7,23},{8,24},{9,... | collective-permute-start | bytes 737288 | tf_op jit(solution)/shard_map/ppermute | solution.py:49
  62.4 11.0 %collective-permute-start.24 = (bf16[192,640]{1,0:T(8,128)(2,1)S(1)}, bf16[192,640]{1,0:T(8,128)(2,1)S(1)}, u32[]{:S(2)}, u32[]{:S(2)}) collective-permute-start(bf16[192,640]{1,0:T(8,128)(2,1)S(1)} %get-tuple-element.59), channel_id=1, source_target_pairs={{0,1},{1,0},{2,3},{3,2},{4,5},{5,4},{6,7},{7,6},{8,9},{9,8},{10,11... | collective-permute-start | bytes 737288 | tf_op jit(solution)/shard_map/ppermute | solution.py:49
  62.6 8.6 %collective-permute-start.25 = (bf16[96,640]{1,0:T(8,128)(2,1)S(1)}, bf16[96,640]{1,0:T(8,128)(2,1)S(1)}, u32[]{:S(2)}, u32[]{:S(2)}) collective-permute-start(bf16[96,640]{1,0:T(8,128)(2,1)S(1)} %get-tuple-element.61), channel_id=1, source_target_pairs={{0,1},{1,0},{2,3},{3,2},{4,5},{5,4},{6,7},{7,6},{8,9},{9,8},{10,11... | collective-permute-start | bytes 368648 | tf_op jit(solution)/shard_map/ppermute | solution.py:49
  64.6 8.0 %collective-permute-start.30 = (bf16[96,640]{1,0:T(8,128)(2,1)S(1)}, bf16[96,640]{1,0:T(8,128)(2,1)S(1)}, u32[]{:S(2)}, u32[]{:S(2)}) collective-permute-start(bf16[96,640]{1,0:T(8,128)(2,1)S(1)} %shard_map.115), channel_id=1, source_target_pairs={{0,16},{1,17},{2,18},{3,19},{4,20},{5,21},{6,22},{7,23},{8,24},{9,... | collective-permute-start | bytes 368648 | tf_op jit(solution)/shard_map/ppermute | solution.py:49
  65.9 16.4 %collective-permute-start.21 = (bf16[192,640]{1,0:T(8,128)(2,1)S(1)}, bf16[192,640]{1,0:T(8,128)(2,1)S(1)}, u32[]{:S(2)}, u32[]{:S(2)}) collective-permute-start(bf16[192,640]{1,0:T(8,128)(2,1)S(1)} %get-tuple-element.55), channel_id=1, source_target_pairs={{0,16},{1,17},{2,18},{3,19},{4,20},{5,21},{6,22},{7,23},{8,28},{9,... | collective-permute-start | bytes 737288 | tf_op jit(solution)/shard_map/ppermute | solution.py:49
  66.7 15.6 %collective-permute-start.14 = (bf16[192,640]{1,0:T(8,128)(2,1)S(1)}, bf16[192,640]{1,0:T(8,128)(2,1)S(1)}, u32[]{:S(2)}, u32[]{:S(2)}) collective-permute-start(bf16[192,640]{1,0:T(8,128)(2,1)S(1)} %get-tuple-element.51), channel_id=1, source_target_pairs={{0,0},{1,1},{2,2},{3,3},{4,4},{5,5},{6,6},{7,7},{8,12},{9,13},{10,... | collective-permute-start | bytes 737288 | tf_op jit(solution)/shard_map/ppermute | solution.py:49
  71.2 11.1 %collective-permute-start.23 = (bf16[192,640]{1,0:T(8,128)(2,1)S(1)}, bf16[192,640]{1,0:T(8,128)(2,1)S(1)}, u32[]{:S(2)}, u32[]{:S(2)}) collective-permute-start(bf16[192,640]{1,0:T(8,128)(2,1)S(1)} %shard_map.110), channel_id=1, source_target_pairs={{0,1},{1,0},{2,3},{3,2},{4,5},{5,4},{6,7},{7,6},{8,13},{9,12},{10,... | collective-permute-start | bytes 737288 | tf_op jit(solution)/shard_map/ppermute | solution.py:49
  73.5 8.8 %collective-permute-start.31 = (bf16[96,640]{1,0:T(8,128)(2,1)S(1)}, bf16[96,640]{1,0:T(8,128)(2,1)S(1)}, u32[]{:S(2)}, u32[]{:S(2)}) collective-permute-start(bf16[96,640]{1,0:T(8,128)(2,1)S(1)} %shard_map.116), channel_id=1, source_target_pairs={{0,2},{1,3},{2,0},{3,1},{4,6},{5,7},{6,4},{7,5},{8,14},{9,15},{10,... | collective-permute-start | bytes 368648 | tf_op jit(solution)/shard_map/ppermute | solution.py:49
  77.6 9.0 %collective-permute-start.27 = (bf16[96,640]{1,0:T(8,128)(2,1)S(1)}, bf16[96,640]{1,0:T(8,128)(2,1)S(1)}, u32[]{:S(2)}, u32[]{:S(2)}) collective-permute-start(bf16[96,640]{1,0:T(8,128)(2,1)S(1)} %shard_map.113), channel_id=1, source_target_pairs={{0,2},{1,3},{2,0},{3,1},{4,6},{5,7},{6,4},{7,5},{8,14},{9,15},{10,... | collective-permute-start | bytes 368648 | tf_op jit(solution)/shard_map/ppermute | solution.py:49
  (18 other events, 116.0 us)

commit v3 on v2

--- a/solution.py
+++ b/solution.py
@@ -12,7 +12,7 @@
 
 floor_score = -1e30
 norm_eps = 1e-05
-EXTRA = 16
+EXTRA = 8
 f32 = jnp.float32
 bf16 = jnp.bfloat16
 VMEM = pl.BlockSpec(memory_space=pltpu.VMEM)
@@ -74,7 +74,7 @@
     return [high, middle, (rest - middle.astype(f32)).astype(bf16)]
 
 
-def prep_body(experts, cap, where_ref, q_in, res_in, ids_in, logit_in, gain_in, q_out, res_out, taken_ref, *refs):
+def prep_body(experts, ff, cap, where_ref, q_in, res_in, ids_in, logit_in, gain_in, q_out, res_out, taken_ref, *refs):
     extra_refs = refs[: 2 if experts == 2 else 1]
     lit_ref, ids_ref, logit_ref, gain_ref, sems = refs[len(extra_refs) :]
     pairs = [(ids_in, ids_ref), (logit_in, logit_ref), (gain_in, gain_ref), (q_in.at[0], q_out), (res_in.at[0], res_out)]
@@ -86,7 +86,7 @@
     slots = taken_ref.shape[1]
     route = as_column(ids_ref[...].astype(f32)).astype(jnp.int32)
     if experts == 2:
-        route = route ^ where_ref[0]
+        route = route ^ (where_ref[0] // ff % experts) ^ (where_ref[0] // (ff * experts) & 1)
     lanes = lax.broadcasted_iota(jnp.int32, (shard, shard), 1)
     rows = lax.broadcasted_iota(jnp.int32, (shard, shard), 0)
     onehot = (lanes == route).astype(f32)
@@ -114,13 +114,13 @@
         c.wait()
 
 
-def attend_body(group, blocks, extras, layout, where_ref, q_ref, res_ref, taken_ref, *refs):
+def attend_body(group, blocks, plane, layout, where_ref, q_ref, res_ref, taken_ref, *refs):
     kv_refs = refs[:blocks]
-    extra_refs = refs[blocks : blocks + extras]
-    stream_ref = refs[blocks + extras]
-    send_refs = refs[blocks + extras + 1 :]
+    extra_refs = refs[blocks : blocks + 1]
+    stream_ref = refs[blocks + 1]
+    send_refs = refs[blocks + 2 :]
     shard = q_ref.shape[0]
-    me = where_ref[0]
+    me = where_ref[0] // plane
     rows = lax.broadcasted_iota(jnp.int32, (shard, shard), 0)
     cols = lax.broadcasted_iota(jnp.int32, (shard, shard), 1)
     nt = (((1,), (1,)), ((), ()))
@@ -148,8 +148,7 @@
     for ref, (at, rows, extra) in zip(send_refs, layout):
         ref[:rows] = send[at : at + rows]
         if extra:
-            own, got = extra_refs[0][...], extra_refs[1][...]
-            ref[rows:] = jnp.concatenate([own[:6], got[3:6], own[9:]], axis=0)
+            ref[rows:] = extra_refs[0][...]
 
 
 def joined(refs, spans):
@@ -157,8 +156,8 @@
     return parts[0] if len(parts) == 1 else jnp.concatenate(parts, axis=0)
 
 
-def whole(ref, row, width):
-    return sum(ref[row + i : row + i + 1, :width].astype(f32) for i in range(3))
+def whole(ref, row, lane, width):
+    return sum(ref[row + i : row + i + 1, lane : lane + width].astype(f32) for i in range(3))
 
 
 def load_body(*refs):
@@ -179,20 +178,22 @@
     )(*[pltpu.with_memory_space_constraint(a, pltpu.HBM) for a in arrays])
 
 
-def join_body(keep_ref, got_ref, out_ref):
+def join_body(keep_ref, got_ref, extra_ref, out_ref):
     cap = got_ref.shape[0]
     out_ref[:cap] = keep_ref[:cap]
     out_ref[cap : 2 * cap] = got_ref[...]
-    out_ref[2 * cap :] = keep_ref[cap:]
-
-
-def mlp_body(spec, lit_of, begun, where_ref, *refs):
+    own, got = keep_ref[cap:], extra_ref[...]
+    both = jnp.concatenate([own[3:6, :HD], got[3:6, :HD], own[3:6, 2 * HD :]], axis=1)
+    out_ref[2 * cap :] = jnp.concatenate([own[:3], both, own[6:]], axis=0)
+
+
+def mlp_body(ff, spec, lit_of, begun, where_ref, *refs):
     refs = list(refs)
     acc_in = [refs.pop(0) for _ in range(3)] if begun else None
     blocks = [([refs.pop(0) for _ in range(n)], spans, gain, i) for n, spans, gain, i in spec]
     lits = [refs.pop(0) for _ in lit_of]
     gates, ups = ([refs.pop(0) for _ in range(2)] for _ in range(2))
-    mine = where_ref[0]
+    mine = lax.rem(where_ref[0], ff)
     g, u, squares = ([None, None], [None, None], None)
     if begun:
         hidden = gates[0].shape[1]
@@ -208,7 +209,7 @@
         wide = joined(arrays, spans).astype(f32)
         quarter = wide.shape[1]
         squares = plus(squares, jnp.sum(wide * wide, axis=1, keepdims=True))
-        x = (wide * whole(arrays[0], gain_row, quarter)).astype(bf16)
+        x = (wide * whole(arrays[0], gain_row, 0, quarter)).astype(bf16)
         part = pl.ds(pl.multiple_of(at * quarter, quarter), quarter)
         for k in range(2):
             g[k] = plus(g[k], jnp.dot(x, gates[k][part, :], preferred_element_type=f32))
@@ -222,7 +223,7 @@
     downs = [refs.pop(0) for _ in range(2)]
     outs = refs
     rows, quarter = outs[0].shape
-    opened = [as_column(whole(ref, row, n)) for ref, (row, n) in zip(lits, lit_of)]
+    opened = [as_column(whole(ref, *place)) for ref, place in zip(lits, lit_of)]
     opened = opened[0] if len(opened) == 1 else jnp.concatenate(opened, axis=0)
     factor = lax.rsqrt(squares / (4 * quarter) + norm_eps) * opened
     act = []
@@ -245,7 +246,7 @@
 def mlp(mine, blocks, weights, begun=None, lits=(), halve=False):
     spec = [(len(arrays), spans, gain, i) for arrays, spans, gain, i in blocks]
     rows, quarter = sum(n for _, _, n in blocks[0][1]), blocks[0][0][0].shape[1]
-    flat = [*(begun or ()), *[a for arrays, *_ in blocks for a in arrays], *[a for a, _, _ in lits]]
+    flat = [*(begun or ()), *[a for arrays, *_ in blocks for a in arrays], *[a for a, *_ in lits]]
     hidden = weights[0].shape[1]
     flops = 2 * rows * quarter * len(blocks) * hidden * 4
     if lits:
@@ -257,7 +258,7 @@
         weights = weights[:4]
     weights = [pltpu.with_memory_space_constraint(w, pltpu.VMEM) for w in weights]
     return kernel(
-        functools.partial(mlp_body, spec, [(row, n) for _, row, n in lits], begun is not None),
+        functools.partial(mlp_body, lax.axis_size("ff"), spec, [tuple(place) for _, *place in lits], begun is not None),
         out,
         [SMEM] + [VMEM] * (len(flat) + len(weights)),
         [VMEM] * len(out),
@@ -318,9 +319,8 @@
 ):
     shard, quarter = query_proj.shape[1:]
     seq, experts = lax.axis_size("seq"), lax.axis_size("exp")
-    sid = lax.axis_index("seq").astype(jnp.int32)[None]
-    eid = lax.axis_index("exp").astype(jnp.int32)[None] ^ (sid & 1)
-    fid = lax.axis_index("ff").astype(jnp.int32)[None]
+    ff = lax.axis_size("ff")
+    place = lax.axis_index(("seq", "exp", "ff")).astype(jnp.int32)[None]
     cap = max(2, 3 * shard // (2 * experts))
     slots = experts * cap
     two = experts == 2
@@ -339,7 +339,7 @@
     kv3 = flip(kv2, seq=1)
     extras = 2 if two else 1
     query, res, taken, *extra, lit = kernel(
-        functools.partial(prep_body, experts, cap),
+        functools.partial(prep_body, experts, ff, cap),
         (
             near((shard, quarter), bf16),
             near((shard, quarter), bf16),
@@ -351,25 +351,23 @@
         (VMEM,) * (4 + extras),
         8,
         scratch=[near((1, shard), jnp.int32), near((1, shard), f32), near((quarter,), f32), dma((5,))],
-    )(eid, far_off(query_proj), far_off(residual), far_off(expert_ids[0, :, 0][None]), far_off(router_logit), far_off(norm_gain))
+    )(place, far_off(query_proj), far_off(residual), far_off(expert_ids[0, :, 0][None]), far_off(router_logit), far_off(norm_gain))
 
     layout = [(0, cap, True), (cap, cap, False)] if two else [(0, slots, False)]
-    if two:
-        extra[1] = flip(extra[1], seq=1)
     stream, *send = kernel(
-        functools.partial(attend_body, HEADS // KVH, seq, extras, layout),
+        functools.partial(attend_body, HEADS // KVH, seq, experts * ff, layout),
         [near((shard, quarter), bf16)] + [near((n + (EXTRA if e else 0), quarter), bf16) for _, n, e in layout],
-        [SMEM] + [VMEM] * (3 + seq + extras),
+        [SMEM] + [VMEM] * (4 + seq),
         (VMEM,) * (1 + len(layout)),
         8,
-    )(sid, query, res, taken, kv, kv1, kv2, kv3, *extra)
+    )(place, query, res, taken, kv, kv1, kv2, kv3, extra[0])
 
     rows = 2 * cap if two else slots
     if two:
         got = flip(send[1], seq=1)
         halves = [send[0], got]
-        block = kernel(join_body, near((rows + EXTRA, quarter), bf16), [VMEM] * 2, VMEM, 4)(*halves)
-        lit_of = ((rows + 3, cap), (rows + 6, cap))
+        block = kernel(join_body, near((rows + EXTRA, quarter), bf16), [VMEM] * 3, VMEM, 4)(*halves, flip(extra[1], seq=1))
+        lit_of = ((rows + 3, 0, cap), (rows + 3, HD, cap))
         spans, gain_row = ((0, 0, cap), (1, 0, cap)), cap
     else:
         block = lax.all_to_all(send[0], "exp", split_axis=0, concat_axis=0, tiled=True)
@@ -377,7 +375,7 @@
         lit = jnp.pad(jnp.stack(split(lit)), ((0, 0), (0, quarter - slots)))
         block = jnp.concatenate([block, extra[0][:3], lit, extra[0][6:]], axis=0)
         halves = [block]
-        lit_of = ((rows + 3, slots),)
+        lit_of = ((rows + 3, 0, slots),)
         spans, gain_row = ((0, 0, rows),), rows
 
     def each(arrays, *args, **bits):
@@ -389,7 +387,7 @@
     own_x = flip(block, two, seq=2)
     own = flip(block, two) if two else block
     partner = each(weights, seq=1)
-    pairs = [w for both in zip(load(weights), load(partner)) for w in both]
+    pairs = [w for both in zip(load(weights), partner) for w in both]
     far = each(sel, ff=1)
     sel_x = each(sel, seq=2)
     non_x = flip(non, seq=2)
@@ -399,19 +397,19 @@
         return [([a], ((0, 0, rows),), rows, i) if not isinstance(a, list) else (a, spans, gain_row, i) for a, i in parts]
 
     def lit_in(array):
-        return [(array, row, n) for row, n in lit_of]
-
-    begun = mlp(fid, blocks((own, 0), (sel, 2), (non, 1)), pairs)
-    p0, p1, p2, p3 = mlp(fid, blocks((far, 3)), pairs, begun, lit_in(own))
-    begun = mlp(fid, blocks((own_x, 0), (sel_x, 2), (non_x, 1)), pairs)
-    o0, o1, o2, *o3 = mlp(fid, blocks((far_x, 3)), pairs, begun, lit_in(own_x), two)
+        return [(array, *place) for place in lit_of]
+
+    begun = mlp(place, blocks((own, 0), (sel, 2), (non, 1)), pairs)
+    p0, p1, p2, *p3 = mlp(place, blocks((far, 3)), pairs, begun, lit_in(own), two)
+    begun = mlp(place, blocks((own_x, 0), (sel_x, 2), (non_x, 1)), pairs)
+    o0, o1, o2, *o3 = mlp(place, blocks((far_x, 3)), pairs, begun, lit_in(own_x), two)
 
     part = cap if two else slots
     order = range(len(o3))
     back_x = each(o3, ff=1)
-    back = flip(p3, ff=1)
+    back = each(p3, ff=1)
     over = each([sum_rows(part, (o2, i * part), (back_x[i], 0)) for i in order], seq=2)
-    last = [sum_rows(part, (p2, i * part), (back, i * part), (over[i], 0)) for i in order]
+    last = [sum_rows(part, (p2, i * part), (back[i], 0), (over[i], 0)) for i in order]
     last = each(last, two, ff=2)
     tot_non = sum_rows(rows, (p1, 0), (flip(o1, seq=2), 0))
     home = flip(p0, two) if two else p0

time: 87.8 us -> 93.4 us (1.064)
  starting transfers between devices: 36.1 us -> 41.1 us
  waiting for transfers between devices: 32.3 us -> 36.4 us
  Pallas kernels: 17.8 us -> 15.4 us
  local copies, waits for them, and re-layouts: 1.09 us -> 0 us
    ppermute x33 -> x34, starting transfers between devices: 36.1 us -> 41.1 us  [flip(): return lax.ppermute(value, axes, pairs)]
    ppermute x33 -> x34, waiting for transfers between devices: 32.3 us -> 36.4 us  [flip(): return lax.ppermute(value, axes, pairs)]
    pallas_call x2 -> x1, Pallas kernels: 4.3 us -> 2.13 us  [load(): kernel(load_body, [pltpu.VMEM(a.shape, a.dtype) for a in arrays], [RAW] *...]
    unnamed x18 -> x0, local copies, waits for them, and re-layouts: 1.09 us -> none
  transfers between devices with their start and end apart: 33 -> 34, of which waited for: 13 -> 16; matrix products, arithmetic and copies ran while one was open for 0% -> 0% of each run, Pallas kernels for 19% -> 16%
where the time goes in v3:
time: 93.4 us; the launch traced here: 93.1 us
  starting transfers between devices  41.1 us (44%)
  waiting for transfers between devices  36.4 us (39%)
  Pallas kernels  15.4 us (16%)
    ppermute x34, starting transfers between devices, flip(): return lax.ppermute(value, axes, pairs)  41.1 us
    ppermute x34, waiting for transfers between devices, flip(): return lax.ppermute(value, axes, pairs)  36.4 us
    pallas_call x4, Pallas kernels, mlp(): kernel(functools.partial(mlp_body, lax.axis_size('ff'), spec, [tuple(plac...  7.46 us
    pallas_call x1, Pallas kernels, load(): kernel(load_body, [pltpu.VMEM(a.shape, a.dtype) for a in arrays], [RAW] *...  2.13 us
    pallas_call x1, Pallas kernels, body(): kernel(functools.partial(attend_body, HEADS // KVH, seq, experts * ff, la...  1.92 us
  transfers between devices with their start and end apart: 34, of which 16 were waited for; matrix products, arithmetic and copies ran while one was open for 0% of the time, Pallas kernels for 16%

profile of v3, /device:TPU:0, one launch (start us, length us, event | category | flops | bytes accessed | tf_op | source)
XLA Modules:
  0.0 93.1 jit_solution(9702438901285465836)
XLA Ops:
  1.8 4.4 %collective-permute-start.1 = (bf16[256,128]{1,0:T(8,128)(2,1)S(1)}, bf16[256,128]{1,0:T(8,128)(2,1)S(1)}, u32[]{:S(2)}, u32[]{:S(2)}) collective-permute-start(bf16[256,128]{1,0:T(8,128)(2,1)S(1)} %shard_map.101.refs_0_), channel_id=1, source_target_pairs={{0,16},{1,17},{2,18},{3,19},{4,20},{5,21},{6,22},{7,23},{8,24},{9,... | collective-permute-start | bytes 196616 | tf_op jit(solution)/shard_map/ppermute | solution.py:49
  6.2 2.1 %collective-permute-start = (bf16[256,128]{1,0:T(8,128)(2,1)S(1)}, bf16[256,128]{1,0:T(8,128)(2,1)S(1)}, u32[]{:S(2)}, u32[]{:S(2)}) collective-permute-start(bf16[256,128]{1,0:T(8,128)(2,1)S(1)} %shard_map.101.refs_0_), channel_id=1, source_target_pairs={{0,8},{1,9},{2,10},{3,11},{4,12},{5,13},{6,14},{7,15},{16,24},{17,... | collective-permute-start | bytes 196616 | tf_op jit(solution)/shard_map/ppermute | solution.py:49
  8.4 1.8 %shard_map.100 = (bf16[128,640]{1,0:T(8,128)(2,1)S(1)}, bf16[128,640]{1,0:T(8,128)(2,1)S(1)}, bf16[128,192]{1,0:T(8,128)(2,1)S(1)}, bf16[8,640]{1,0:T(8,128)(2,1...) custom-call(s32[1]{0:T(128)} %bitcast.where_ref, bf16[1,128,640]{2,1,0:T(8,128)(2,1)} %q_in.1, ...), custom_call_target="tpu_custom_call" | custom-call | tf_op jit(solution)/shard_map/pallas_call | solution.py:341
  10.3 1.9 %shard_map.102 = (bf16[128,640]{1,0:T(8,128)(2,1)S(1)}, bf16[104,640]{1,0:T(8,128)(2,1)S(1)}, bf16[96,640]{1,0:T(8,128)(2,1)S(1)}) custom-call(s32[1]{0:T(128)} %bitcast.where_ref, bf16[128,640]{1,0:T(8,128)(2,1)S(1)} %get-tuple-element.32.q_ref, bf16[128,640]{1,0:T(8,128)(2,1)S(1)} %get-tuple-element.33.res_ref, ...), custom_call_target="tpu_custom_call" | custom-call | tf_op jit(solution)/shard_map/pallas_call | solution.py:357
  13.9 2.6 %collective-permute-start.6 = (bf16[104,640]{1,0:T(8,128)(2,1)S(1)}, bf16[104,640]{1,0:T(8,128)(2,1)S(1)}, u32[]{:S(2)}, u32[]{:S(2)}) collective-permute-start(bf16[104,640]{1,0:T(8,128)(2,1)S(1)} %get-tuple-element.37.keep_ref), channel_id=1, source_target_pairs={{0,2},{1,3},{2,0},{3,1},{4,6},{5,7},{6,4},{7,5},{8,14},{9,15},{10,... | collective-permute-start | bytes 399368 | tf_op jit(solution)/shard_map/ppermute | solution.py:49
  16.8 9.7 %collective-permute-done.6.refs_1_ = bf16[104,640]{1,0:T(8,128)(2,1)S(1)} collective-permute-done((bf16[104,640]{1,0:T(8,128)(2,1)S(1)}, bf16[104,640]{1,0:T(8,128)(2,1)S(1)}, u32[]{:S(2)}, u32[]{:S(2)}) %collective-permute-start.6) | collective-permute-done | bytes 133152 | tf_op jit(solution)/shard_map/ppermute | solution.py:49
  26.5 2.3 %collective-permute-start.16 = (bf16[104,640]{1,0:T(8,128)(2,1)S(1)}, bf16[104,640]{1,0:T(8,128)(2,1)S(1)}, u32[]{:S(2)}, u32[]{:S(2)}) collective-permute-start(bf16[104,640]{1,0:T(8,128)(2,1)S(1)} %collective-permute-done.6.refs_1_), channel_id=1, source_target_pairs={{0,16},{1,17},{2,18},{3,19},{4,20},{5,21},{6,22},{7,23},{8,24},{9,... | collective-permute-start | bytes 399368 | tf_op jit(solution)/shard_map/ppermute | solution.py:49
  30.0 1.8 %collective-permute-done.16.refs_1_ = bf16[104,640]{1,0:T(8,128)(2,1)S(1)} collective-permute-done((bf16[104,640]{1,0:T(8,128)(2,1)S(1)}, bf16[104,640]{1,0:T(8,128)(2,1)S(1)}, u32[]{:S(2)}, u32[]{:S(2)}) %collective-permute-start.16) | collective-permute-done | bytes 133152 | tf_op jit(solution)/shard_map/ppermute | solution.py:49
  31.8 2.0 %collective-permute-start.17 = (bf16[96,640]{1,0:T(8,128)(2,1)S(1)}, bf16[96,640]{1,0:T(8,128)(2,1)S(1)}, u32[]{:S(2)}, u32[]{:S(2)}) collective-permute-start(bf16[96,640]{1,0:T(8,128)(2,1)S(1)} %collective-permute-done.7.refs_2_), channel_id=1, source_target_pairs={{0,16},{1,17},{2,18},{3,19},{4,20},{5,21},{6,22},{7,23},{8,24},{9,... | collective-permute-start | bytes 368648 | tf_op jit(solution)/shard_map/ppermute | solution.py:49
  33.8 2.9 %collective-permute-done.17.refs_2_ = bf16[96,640]{1,0:T(8,128)(2,1)S(1)} collective-permute-done((bf16[96,640]{1,0:T(8,128)(2,1)S(1)}, bf16[96,640]{1,0:T(8,128)(2,1)S(1)}, u32[]{:S(2)}, u32[]{:S(2)}) %collective-permute-start.17) | collective-permute-done | bytes 122912 | tf_op jit(solution)/shard_map/ppermute | solution.py:49
  36.6 2.0 %collective-permute-start.15 = (bf16[200,640]{1,0:T(8,128)(2,1)S(1)}, bf16[200,640]{1,0:T(8,128)(2,1)S(1)}, u32[]{:S(2)}, u32[]{:S(2)}) collective-permute-start(bf16[200,640]{1,0:T(8,128)(2,1)S(1)} %shard_map.103), channel_id=1, source_target_pairs={{0,16},{1,17},{2,18},{3,19},{4,20},{5,21},{6,22},{7,23},{8,28},{9,... | collective-permute-start | bytes 768008 | tf_op jit(solution)/shard_map/ppermute | solution.py:49
  38.7 1.7 %collective-permute-start.18 = (bf16[200,640]{1,0:T(8,128)(2,1)S(1)}, bf16[200,640]{1,0:T(8,128)(2,1)S(1)}, u32[]{:S(2)}, u32[]{:S(2)}) collective-permute-start(bf16[200,640]{1,0:T(8,128)(2,1)S(1)} %collective-permute-done.8.refs_3_), channel_id=1, source_target_pairs={{0,16},{1,17},{2,18},{3,19},{4,20},{5,21},{6,22},{7,23},{8,24},{9,... | collective-permute-start | bytes 768008 | tf_op jit(solution)/shard_map/ppermute | solution.py:49
  40.4 5.3 %collective-permute-done.15.refs_0_.refs_5_.refs_6_ = bf16[200,640]{1,0:T(8,128)(2,1)S(1)} collective-permute-done((bf16[200,640]{1,0:T(8,128)(2,1)S(1)}, bf16[200,640]{1,0:T(8,128)(2,1)S(1)}, u32[]{:S(2)}, u32[]{:S(2)}) %collective-permute-start.15) | collective-permute-done | bytes 256032 | tf_op jit(solution)/shard_map/ppermute | solution.py:49
  46.4 4.1 %collective-permute-done.18.refs_3_ = bf16[200,640]{1,0:T(8,128)(2,1)S(1)} collective-permute-done((bf16[200,640]{1,0:T(8,128)(2,1)S(1)}, bf16[200,640]{1,0:T(8,128)(2,1)S(1)}, u32[]{:S(2)}, u32[]{:S(2)}) %collective-permute-start.18) | collective-permute-done | bytes 256032 | tf_op jit(solution)/shard_map/ppermute | solution.py:49
  50.5 2.0 %collective-permute-start.20 = (bf16[96,640]{1,0:T(8,128)(2,1)S(1)}, bf16[96,640]{1,0:T(8,128)(2,1)S(1)}, u32[]{:S(2)}, u32[]{:S(2)}) collective-permute-start(bf16[96,640]{1,0:T(8,128)(2,1)S(1)} %collective-permute-done.17.refs_2_), channel_id=1, source_target_pairs={{0,1},{1,0},{2,3},{3,2},{4,5},{5,4},{6,7},{7,6},{8,9},{9,8},{10,11... | collective-permute-start | bytes 368648 | tf_op jit(solution)/shard_map/ppermute | solution.py:49
  52.5 2.1 %shard_map.104 = (bf16[2560,256]{1,0:T(8,128)(2,1)S(1)}, bf16[2560,256]{1,0:T(8,128)(2,1)S(1)}, bf16[256,2560]{1,0:T(8,128)(2,1)S(1)}) custom-call(bf16[2560,256]{1,0:T(8,128)(2,1)} %bitcast.6, bf16[2560,256]{1,0:T(8,128)(2,1)} %bitcast.8, bf16[256,2560]{1,0:T(8,128)(2,1)} %bitcast.10), custom_call_target="tpu_custom_call" | custom-call | tf_op jit(solution)/shard_map/pallas_call | solution.py:175
  57.9 1.6 %collective-permute-done.20.refs_4_ = bf16[96,640]{1,0:T(8,128)(2,1)S(1)} collective-permute-done((bf16[96,640]{1,0:T(8,128)(2,1)S(1)}, bf16[96,640]{1,0:T(8,128)(2,1)S(1)}, u32[]{:S(2)}, u32[]{:S(2)}) %collective-permute-start.20) | collective-permute-done | bytes 122912 | tf_op jit(solution)/shard_map/ppermute | solution.py:49
  59.5 2.6 %shard_map.108 = (bf16[192,640]{1,0:T(8,128)(2,1)S(1)}, bf16[192,640]{1,0:T(8,128)(2,1)S(1)}, bf16[192,640]{1,0:T(8,128)(2,1)S(1)}, bf16[96,640]{1,0:T(8,128)(2,1)S(1)}, bf16[96,640]{1,0:T(8,128)(2,1)S(1)}) custom-call(s32[1]{0:T(128)} %bitcast.where_ref, f32[192,512]{1,0:T(8,128)S(1)} %get-tuple-element.47.refs_0_, ...), custom_call_target="tpu_custom_call" | custom-call | flops 754974720 | bytes 8388608 | tf_op jit(solution)/shard_map/pallas_call | solution.py:260
  63.7 1.7 %collective-permute-start.30 = (bf16[96,640]{1,0:T(8,128)(2,1)S(1)}, bf16[96,640]{1,0:T(8,128)(2,1)S(1)}, u32[]{:S(2)}, u32[]{:S(2)}) collective-permute-start(bf16[96,640]{1,0:T(8,128)(2,1)S(1)} %get-tuple-element.58), channel_id=1, source_target_pairs={{0,1},{1,0},{2,3},{3,2},{4,5},{5,4},{6,7},{7,6},{8,9},{9,8},{10,11... | collective-permute-start | bytes 368648 | tf_op jit(solution)/shard_map/ppermute | solution.py:49
  66.5 2.6 %shard_map.106 = (bf16[192,640]{1,0:T(8,128)(2,1)S(1)}, bf16[192,640]{1,0:T(8,128)(2,1)S(1)}, bf16[192,640]{1,0:T(8,128)(2,1)S(1)}, bf16[96,640]{1,0:T(8,128)(2,1)S(1)}, bf16[96,640]{1,0:T(8,128)(2,1)S(1)}) custom-call(s32[1]{0:T(128)} %bitcast.where_ref, f32[192,512]{1,0:T(8,128)S(1)} %get-tuple-element.42.refs_0_, ...), custom_call_target="tpu_custom_call" | custom-call | flops 754974720 | bytes 8388608 | tf_op jit(solution)/shard_map/pallas_call | solution.py:260
  75.7 1.5 %collective-permute-done.31.refs_2_ = bf16[96,640]{1,0:T(8,128)(2,1)S(1)} collective-permute-done((bf16[96,640]{1,0:T(8,128)(2,1)S(1)}, bf16[96,640]{1,0:T(8,128)(2,1)S(1)}, u32[]{:S(2)}, u32[]{:S(2)}) %collective-permute-start.31) | collective-permute-done | bytes 122912 | tf_op jit(solution)/shard_map/ppermute | solution.py:49
  78.2 3.8 %collective-permute-start.32 = (bf16[96,640]{1,0:T(8,128)(2,1)S(1)}, bf16[96,640]{1,0:T(8,128)(2,1)S(1)}, u32[]{:S(2)}, u32[]{:S(2)}) collective-permute-start(bf16[96,640]{1,0:T(8,128)(2,1)S(1)} %shard_map.115), channel_id=1, source_target_pairs={{0,2},{1,3},{2,0},{3,1},{4,6},{5,7},{6,4},{7,5},{8,14},{9,15},{10,... | collective-permute-start | bytes 368648 | tf_op jit(solution)/shard_map/ppermute | solution.py:49
  82.7 3.5 %collective-permute-start.27 = (bf16[96,640]{1,0:T(8,128)(2,1)S(1)}, bf16[96,640]{1,0:T(8,128)(2,1)S(1)}, u32[]{:S(2)}, u32[]{:S(2)}) collective-permute-start(bf16[96,640]{1,0:T(8,128)(2,1)S(1)} %shard_map.112), channel_id=1, source_target_pairs={{0,2},{1,3},{2,0},{3,1},{4,6},{5,7},{6,4},{7,5},{8,14},{9,15},{10,... | collective-permute-start | bytes 368648 | tf_op jit(solution)/shard_map/ppermute | solution.py:49
  86.2 4.2 %collective-permute-done.32 = bf16[96,640]{1,0:T(8,128)(2,1)S(1)} collective-permute-done((bf16[96,640]{1,0:T(8,128)(2,1)S(1)}, bf16[96,640]{1,0:T(8,128)(2,1)S(1)}, u32[]{:S(2)}, u32[]{:S(2)}) %collective-permute-start.32) | collective-permute-done | bytes 122912 | tf_op jit(solution)/shard_map/ppermute | solution.py:49
  (61 shorter events, 22.5 us)
Async XLA Ops:
  0.0 50.5 %collective-permute-start.9 = (bf16[2560,256]{1,0:T(8,128)(2,1)}, bf16[2560,256]{1,0:T(8,128)(2,1)S(1)}, u32[]{:S(2)}, u32[]{:S(2)}) collective-permute-start(bf16[2560,256]{1,0:T(8,128)(2,1)} %bitcast.5), channel_id=1, source_target_pairs={{0,8},{1,9},{2,10},{3,11},{4,12},{5,13},{6,14},{7,15},{8,0},{9,1},... | collective-permute-start | bytes 3932168 | tf_op jit(solution)/shard_map/ppermute | solution.py:49
  0.5 54.2 %collective-permute-start.10 = (bf16[2560,256]{1,0:T(8,128)(2,1)}, bf16[2560,256]{1,0:T(8,128)(2,1)S(1)}, u32[]{:S(2)}, u32[]{:S(2)}) collective-permute-start(bf16[2560,256]{1,0:T(8,128)(2,1)} %bitcast.7), channel_id=1, source_target_pairs={{0,8},{1,9},{2,10},{3,11},{4,12},{5,13},{6,14},{7,15},{8,0},{9,1},... | collective-permute-start | bytes 3932168 | tf_op jit(solution)/shard_map/ppermute | solution.py:49
  0.5 59.0 %collective-permute-start.13 = (bf16[256,2560]{1,0:T(8,128)(2,1)}, bf16[256,2560]{1,0:T(8,128)(2,1)}, u32[]{:S(2)}, u32[]{:S(2)}) collective-permute-start(bf16[256,2560]{1,0:T(8,128)(2,1)} %bitcast.9), channel_id=1, source_target_pairs={{0,8},{1,9},{2,10},{3,11},{4,12},{5,13},{6,14},{7,15},{8,0},{9,1},... | collective-permute-start | bytes 3932168 | tf_op jit(solution)/shard_map/ppermute | solution.py:49
  1.8 6.5 %collective-permute-start.1 = (bf16[256,128]{1,0:T(8,128)(2,1)S(1)}, bf16[256,128]{1,0:T(8,128)(2,1)S(1)}, u32[]{:S(2)}, u32[]{:S(2)}) collective-permute-start(bf16[256,128]{1,0:T(8,128)(2,1)S(1)} %shard_map.101.refs_0_), channel_id=1, source_target_pairs={{0,16},{1,17},{2,18},{3,19},{4,20},{5,21},{6,22},{7,23},{8,24},{9,... | collective-permute-start | bytes 196616 | tf_op jit(solution)/shard_map/ppermute | solution.py:49
  13.9 12.6 %collective-permute-start.6 = (bf16[104,640]{1,0:T(8,128)(2,1)S(1)}, bf16[104,640]{1,0:T(8,128)(2,1)S(1)}, u32[]{:S(2)}, u32[]{:S(2)}) collective-permute-start(bf16[104,640]{1,0:T(8,128)(2,1)S(1)} %get-tuple-element.37.keep_ref), channel_id=1, source_target_pairs={{0,2},{1,3},{2,0},{3,1},{4,6},{5,7},{6,4},{7,5},{8,14},{9,15},{10,... | collective-permute-start | bytes 399368 | tf_op jit(solution)/shard_map/ppermute | solution.py:49
  16.5 12.7 %collective-permute-start.7 = (bf16[96,640]{1,0:T(8,128)(2,1)S(1)}, bf16[96,640]{1,0:T(8,128)(2,1)S(1)}, u32[]{:S(2)}, u32[]{:S(2)}) collective-permute-start(bf16[96,640]{1,0:T(8,128)(2,1)S(1)} %collective-permute-done.3.got_ref), channel_id=1, source_target_pairs={{0,2},{1,3},{2,0},{3,1},{4,6},{5,7},{6,4},{7,5},{8,14},{9,15},{10,... | collective-permute-start | bytes 368648 | tf_op jit(solution)/shard_map/ppermute | solution.py:49
  29.2 9.5 %collective-permute-start.8 = (bf16[200,640]{1,0:T(8,128)(2,1)S(1)}, bf16[200,640]{1,0:T(8,128)(2,1)S(1)}, u32[]{:S(2)}, u32[]{:S(2)}) collective-permute-start(bf16[200,640]{1,0:T(8,128)(2,1)S(1)} %shard_map.103), channel_id=1, source_target_pairs={{0,1},{1,0},{2,3},{3,2},{4,5},{5,4},{6,7},{7,6},{8,13},{9,12},{10,... | collective-permute-start | bytes 768008 | tf_op jit(solution)/shard_map/ppermute | solution.py:49
  36.6 9.0 %collective-permute-start.15 = (bf16[200,640]{1,0:T(8,128)(2,1)S(1)}, bf16[200,640]{1,0:T(8,128)(2,1)S(1)}, u32[]{:S(2)}, u32[]{:S(2)}) collective-permute-start(bf16[200,640]{1,0:T(8,128)(2,1)S(1)} %shard_map.103), channel_id=1, source_target_pairs={{0,16},{1,17},{2,18},{3,19},{4,20},{5,21},{6,22},{7,23},{8,28},{9,... | collective-permute-start | bytes 768008 | tf_op jit(solution)/shard_map/ppermute | solution.py:49
  38.7 11.8 %collective-permute-start.18 = (bf16[200,640]{1,0:T(8,128)(2,1)S(1)}, bf16[200,640]{1,0:T(8,128)(2,1)S(1)}, u32[]{:S(2)}, u32[]{:S(2)}) collective-permute-start(bf16[200,640]{1,0:T(8,128)(2,1)S(1)} %collective-permute-done.8.refs_3_), channel_id=1, source_target_pairs={{0,16},{1,17},{2,18},{3,19},{4,20},{5,21},{6,22},{7,23},{8,24},{9,... | collective-permute-start | bytes 768008 | tf_op jit(solution)/shard_map/ppermute | solution.py:49
  45.7 18.0 %collective-permute-start.5 = (bf16[200,640]{1,0:T(8,128)(2,1)S(1)}, bf16[200,640]{1,0:T(8,128)(2,1)S(1)}, u32[]{:S(2)}, u32[]{:S(2)}) collective-permute-start(bf16[200,640]{1,0:T(8,128)(2,1)S(1)} %shard_map.103), channel_id=1, source_target_pairs={{0,0},{1,1},{2,2},{3,3},{4,4},{5,5},{6,6},{7,7},{8,12},{9,13},{10,... | collective-permute-start | bytes 768008 | tf_op jit(solution)/shard_map/ppermute | solution.py:49
  50.5 6.4 %collective-permute-start.19 = (bf16[104,640]{1,0:T(8,128)(2,1)S(1)}, bf16[104,640]{1,0:T(8,128)(2,1)S(1)}, u32[]{:S(2)}, u32[]{:S(2)}) collective-permute-start(bf16[104,640]{1,0:T(8,128)(2,1)S(1)} %collective-permute-done.16.refs_1_), channel_id=1, source_target_pairs={{0,1},{1,0},{2,3},{3,2},{4,5},{5,4},{6,7},{7,6},{8,9},{9,8},{10,11... | collective-permute-start | bytes 399368 | tf_op jit(solution)/shard_map/ppermute | solution.py:49
  50.5 9.0 %collective-permute-start.20 = (bf16[96,640]{1,0:T(8,128)(2,1)S(1)}, bf16[96,640]{1,0:T(8,128)(2,1)S(1)}, u32[]{:S(2)}, u32[]{:S(2)}) collective-permute-start(bf16[96,640]{1,0:T(8,128)(2,1)S(1)} %collective-permute-done.17.refs_2_), channel_id=1, source_target_pairs={{0,1},{1,0},{2,3},{3,2},{4,5},{5,4},{6,7},{7,6},{8,9},{9,8},{10,11... | collective-permute-start | bytes 368648 | tf_op jit(solution)/shard_map/ppermute | solution.py:49
  54.7 11.9 %collective-permute-start.11 = (bf16[104,640]{1,0:T(8,128)(2,1)S(1)}, bf16[104,640]{1,0:T(8,128)(2,1)S(1)}, u32[]{:S(2)}, u32[]{:S(2)}) collective-permute-start(bf16[104,640]{1,0:T(8,128)(2,1)S(1)} %collective-permute-done.6.refs_1_), channel_id=1, source_target_pairs={{0,1},{1,0},{2,3},{3,2},{4,5},{5,4},{6,7},{7,6},{8,9},{9,8},{10,11... | collective-permute-start | bytes 399368 | tf_op jit(solution)/shard_map/ppermute | solution.py:49
  56.9 9.6 %collective-permute-start.12 = (bf16[96,640]{1,0:T(8,128)(2,1)S(1)}, bf16[96,640]{1,0:T(8,128)(2,1)S(1)}, u32[]{:S(2)}, u32[]{:S(2)}) collective-permute-start(bf16[96,640]{1,0:T(8,128)(2,1)S(1)} %collective-permute-done.7.refs_2_), channel_id=1, source_target_pairs={{0,1},{1,0},{2,3},{3,2},{4,5},{5,4},{6,7},{7,6},{8,9},{9,8},{10,11... | collective-permute-start | bytes 368648 | tf_op jit(solution)/shard_map/ppermute | solution.py:49
  62.2 9.7 %collective-permute-start.22 = (bf16[192,640]{1,0:T(8,128)(2,1)S(1)}, bf16[192,640]{1,0:T(8,128)(2,1)S(1)}, u32[]{:S(2)}, u32[]{:S(2)}) collective-permute-start(bf16[192,640]{1,0:T(8,128)(2,1)S(1)} %get-tuple-element.52), channel_id=1, source_target_pairs={{0,16},{1,17},{2,18},{3,19},{4,20},{5,21},{6,22},{7,23},{8,24},{9,... | collective-permute-start | bytes 737288 | tf_op jit(solution)/shard_map/ppermute | solution.py:49
  63.4 9.6 %collective-permute-start.25 = (bf16[96,640]{1,0:T(8,128)(2,1)S(1)}, bf16[96,640]{1,0:T(8,128)(2,1)S(1)}, u32[]{:S(2)}, u32[]{:S(2)}) collective-permute-start(bf16[96,640]{1,0:T(8,128)(2,1)S(1)} %get-tuple-element.56), channel_id=1, source_target_pairs={{0,1},{1,0},{2,3},{3,2},{4,5},{5,4},{6,7},{7,6},{8,9},{9,8},{10,11... | collective-permute-start | bytes 368648 | tf_op jit(solution)/shard_map/ppermute | solution.py:49
  63.7 7.2 %collective-permute-start.30 = (bf16[96,640]{1,0:T(8,128)(2,1)S(1)}, bf16[96,640]{1,0:T(8,128)(2,1)S(1)}, u32[]{:S(2)}, u32[]{:S(2)}) collective-permute-start(bf16[96,640]{1,0:T(8,128)(2,1)S(1)} %get-tuple-element.58), channel_id=1, source_target_pairs={{0,1},{1,0},{2,3},{3,2},{4,5},{5,4},{6,7},{7,6},{8,9},{9,8},{10,11... | collective-permute-start | bytes 368648 | tf_op jit(solution)/shard_map/ppermute | solution.py:49
  69.6 20.8 %collective-permute-start.14 = (bf16[192,640]{1,0:T(8,128)(2,1)S(1)}, bf16[192,640]{1,0:T(8,128)(2,1)S(1)}, u32[]{:S(2)}, u32[]{:S(2)}) collective-permute-start(bf16[192,640]{1,0:T(8,128)(2,1)S(1)} %get-tuple-element.46), channel_id=1, source_target_pairs={{0,0},{1,1},{2,2},{3,3},{4,4},{5,5},{6,6},{7,7},{8,12},{9,13},{10,... | collective-permute-start | bytes 737288 | tf_op jit(solution)/shard_map/ppermute | solution.py:49
  70.9 6.3 %collective-permute-start.31 = (bf16[96,640]{1,0:T(8,128)(2,1)S(1)}, bf16[96,640]{1,0:T(8,128)(2,1)S(1)}, u32[]{:S(2)}, u32[]{:S(2)}) collective-permute-start(bf16[96,640]{1,0:T(8,128)(2,1)S(1)} %shard_map.114), channel_id=1, source_target_pairs={{0,16},{1,17},{2,18},{3,19},{4,20},{5,21},{6,22},{7,23},{8,24},{9,... | collective-permute-start | bytes 368648 | tf_op jit(solution)/shard_map/ppermute | solution.py:49
  71.9 6.4 %collective-permute-start.24 = (bf16[96,640]{1,0:T(8,128)(2,1)S(1)}, bf16[96,640]{1,0:T(8,128)(2,1)S(1)}, u32[]{:S(2)}, u32[]{:S(2)}) collective-permute-start(bf16[96,640]{1,0:T(8,128)(2,1)S(1)} %get-tuple-element.54), channel_id=1, source_target_pairs={{0,1},{1,0},{2,3},{3,2},{4,5},{5,4},{6,7},{7,6},{8,9},{9,8},{10,11... | collective-permute-start | bytes 368648 | tf_op jit(solution)/shard_map/ppermute | solution.py:49
  73.0 17.4 %collective-permute-start.21 = (bf16[192,640]{1,0:T(8,128)(2,1)S(1)}, bf16[192,640]{1,0:T(8,128)(2,1)S(1)}, u32[]{:S(2)}, u32[]{:S(2)}) collective-permute-start(bf16[192,640]{1,0:T(8,128)(2,1)S(1)} %get-tuple-element.50), channel_id=1, source_target_pairs={{0,16},{1,17},{2,18},{3,19},{4,20},{5,21},{6,22},{7,23},{8,28},{9,... | collective-permute-start | bytes 737288 | tf_op jit(solution)/shard_map/ppermute | solution.py:49
  74.7 15.7 %collective-permute-start.23 = (bf16[192,640]{1,0:T(8,128)(2,1)S(1)}, bf16[192,640]{1,0:T(8,128)(2,1)S(1)}, u32[]{:S(2)}, u32[]{:S(2)}) collective-permute-start(bf16[192,640]{1,0:T(8,128)(2,1)S(1)} %shard_map.109), channel_id=1, source_target_pairs={{0,1},{1,0},{2,3},{3,2},{4,5},{5,4},{6,7},{7,6},{8,13},{9,12},{10,... | collective-permute-start | bytes 737288 | tf_op jit(solution)/shard_map/ppermute | solution.py:49
  78.2 12.1 %collective-permute-start.32 = (bf16[96,640]{1,0:T(8,128)(2,1)S(1)}, bf16[96,640]{1,0:T(8,128)(2,1)S(1)}, u32[]{:S(2)}, u32[]{:S(2)}) collective-permute-start(bf16[96,640]{1,0:T(8,128)(2,1)S(1)} %shard_map.115), channel_id=1, source_target_pairs={{0,2},{1,3},{2,0},{3,1},{4,6},{5,7},{6,4},{7,5},{8,14},{9,15},{10,... | collective-permute-start | bytes 368648 | tf_op jit(solution)/shard_map/ppermute | solution.py:49
  82.7 9.5 %collective-permute-start.27 = (bf16[96,640]{1,0:T(8,128)(2,1)S(1)}, bf16[96,640]{1,0:T(8,128)(2,1)S(1)}, u32[]{:S(2)}, u32[]{:S(2)}) collective-permute-start(bf16[96,640]{1,0:T(8,128)(2,1)S(1)} %shard_map.112), channel_id=1, source_target_pairs={{0,2},{1,3},{2,0},{3,1},{4,6},{5,7},{6,4},{7,5},{8,14},{9,15},{10,... | collective-permute-start | bytes 368648 | tf_op jit(solution)/shard_map/ppermute | solution.py:49
  (10 other events, 36.0 us)

commit v4 on v3

--- a/solution.py
+++ b/solution.py
@@ -32,7 +32,7 @@
     )
 
 
-def flip(value, cross=False, later=False, seq=0, exp=0, ff=0):
+def flip(value, cross=False, later=None, seq=0, exp=0, ff=0):
     axes = ("seq", "exp", "ff")
     sizes = [lax.axis_size(axis) for axis in axes]
 
@@ -44,7 +44,7 @@
         for e in range(sizes[1]):
             for f in range(sizes[2]):
                 turn = exp ^ (1 if cross and s % 2 else 0)
-                if not later or s < s ^ seq:
+                if later is None or s ^ seq ^ later < s ^ seq:
                     pairs.append((flat(s, e, f), flat(s ^ seq, e ^ turn, f ^ ff)))
     return lax.ppermute(value, axes, pairs)
 
@@ -334,8 +334,8 @@
     kv = kernel(
         pack_body, near((2 * shard, key_proj.shape[2]), bf16), [RAW] * 2, VMEM, 4, scratch=[dma((2,))],
     )(far_off(key_proj), far_off(value_proj))
-    kv2 = flip(kv, later=True, seq=2)
-    kv1 = flip(kv, later=True, seq=1)
+    kv2 = flip(kv, later=2, seq=2)
+    kv1 = flip(kv, later=1, seq=1)
     kv3 = flip(kv2, seq=1)
     extras = 2 if two else 1
     query, res, taken, *extra, lit = kernel(

time: 93.4 us -> 93.4 us (level)
  no operation moved by 1% of the time
where the time goes in v4:
time: 93.4 us; the launch traced here: 93.1 us
  starting transfers between devices  41.1 us (44%)
  waiting for transfers between devices  36.4 us (39%)
  Pallas kernels  15.4 us (16%)
    ppermute x34, starting transfers between devices, flip(): return lax.ppermute(value, axes, pairs)  41.1 us
    ppermute x34, waiting for transfers between devices, flip(): return lax.ppermute(value, axes, pairs)  36.4 us
    pallas_call x4, Pallas kernels, mlp(): kernel(functools.partial(mlp_body, lax.axis_size('ff'), spec, [tuple(plac...  7.46 us
    pallas_call x1, Pallas kernels, load(): kernel(load_body, [pltpu.VMEM(a.shape, a.dtype) for a in arrays], [RAW] *...  2.13 us
    pallas_call x1, Pallas kernels, body(): kernel(functools.partial(attend_body, HEADS // KVH, seq, experts * ff, la...  1.92 us
  transfers between devices with their start and end apart: 34, of which 16 were waited for; matrix products, arithmetic and copies ran while one was open for 0% of the time, Pallas kernels for 16%

profile of v4, /device:TPU:0, one launch (start us, length us, event | category | flops | bytes accessed | tf_op | source)
XLA Modules:
  0.0 93.1 jit_solution(9702438901285465836)
XLA Ops:
  1.8 4.4 %collective-permute-start.1 = (bf16[256,128]{1,0:T(8,128)(2,1)S(1)}, bf16[256,128]{1,0:T(8,128)(2,1)S(1)}, u32[]{:S(2)}, u32[]{:S(2)}) collective-permute-start(bf16[256,128]{1,0:T(8,128)(2,1)S(1)} %shard_map.101.refs_0_), channel_id=1, source_target_pairs={{0,16},{1,17},{2,18},{3,19},{4,20},{5,21},{6,22},{7,23},{8,24},{9,... | collective-permute-start | bytes 196616 | tf_op jit(solution)/shard_map/ppermute | solution.py:49
  6.2 2.1 %collective-permute-start = (bf16[256,128]{1,0:T(8,128)(2,1)S(1)}, bf16[256,128]{1,0:T(8,128)(2,1)S(1)}, u32[]{:S(2)}, u32[]{:S(2)}) collective-permute-start(bf16[256,128]{1,0:T(8,128)(2,1)S(1)} %shard_map.101.refs_0_), channel_id=1, source_target_pairs={{0,8},{1,9},{2,10},{3,11},{4,12},{5,13},{6,14},{7,15},{16,24},{17,... | collective-permute-start | bytes 196616 | tf_op jit(solution)/shard_map/ppermute | solution.py:49
  8.4 1.8 %shard_map.100 = (bf16[128,640]{1,0:T(8,128)(2,1)S(1)}, bf16[128,640]{1,0:T(8,128)(2,1)S(1)}, bf16[128,192]{1,0:T(8,128)(2,1)S(1)}, bf16[8,640]{1,0:T(8,128)(2,1...) custom-call(s32[1]{0:T(128)} %bitcast.where_ref, bf16[1,128,640]{2,1,0:T(8,128)(2,1)} %q_in.1, ...), custom_call_target="tpu_custom_call" | custom-call | tf_op jit(solution)/shard_map/pallas_call | solution.py:341
  10.3 1.9 %shard_map.102 = (bf16[128,640]{1,0:T(8,128)(2,1)S(1)}, bf16[104,640]{1,0:T(8,128)(2,1)S(1)}, bf16[96,640]{1,0:T(8,128)(2,1)S(1)}) custom-call(s32[1]{0:T(128)} %bitcast.where_ref, bf16[128,640]{1,0:T(8,128)(2,1)S(1)} %get-tuple-element.32.q_ref, bf16[128,640]{1,0:T(8,128)(2,1)S(1)} %get-tuple-element.33.res_ref, ...), custom_call_target="tpu_custom_call" | custom-call | tf_op jit(solution)/shard_map/pallas_call | solution.py:357
  13.9 2.6 %collective-permute-start.6 = (bf16[104,640]{1,0:T(8,128)(2,1)S(1)}, bf16[104,640]{1,0:T(8,128)(2,1)S(1)}, u32[]{:S(2)}, u32[]{:S(2)}) collective-permute-start(bf16[104,640]{1,0:T(8,128)(2,1)S(1)} %get-tuple-element.37.keep_ref), channel_id=1, source_target_pairs={{0,2},{1,3},{2,0},{3,1},{4,6},{5,7},{6,4},{7,5},{8,14},{9,15},{10,... | collective-permute-start | bytes 399368 | tf_op jit(solution)/shard_map/ppermute | solution.py:49
  16.8 9.7 %collective-permute-done.6.refs_1_ = bf16[104,640]{1,0:T(8,128)(2,1)S(1)} collective-permute-done((bf16[104,640]{1,0:T(8,128)(2,1)S(1)}, bf16[104,640]{1,0:T(8,128)(2,1)S(1)}, u32[]{:S(2)}, u32[]{:S(2)}) %collective-permute-start.6) | collective-permute-done | bytes 133152 | tf_op jit(solution)/shard_map/ppermute | solution.py:49
  26.5 2.3 %collective-permute-start.16 = (bf16[104,640]{1,0:T(8,128)(2,1)S(1)}, bf16[104,640]{1,0:T(8,128)(2,1)S(1)}, u32[]{:S(2)}, u32[]{:S(2)}) collective-permute-start(bf16[104,640]{1,0:T(8,128)(2,1)S(1)} %collective-permute-done.6.refs_1_), channel_id=1, source_target_pairs={{0,16},{1,17},{2,18},{3,19},{4,20},{5,21},{6,22},{7,23},{8,24},{9,... | collective-permute-start | bytes 399368 | tf_op jit(solution)/shard_map/ppermute | solution.py:49
  30.0 1.8 %collective-permute-done.16.refs_1_ = bf16[104,640]{1,0:T(8,128)(2,1)S(1)} collective-permute-done((bf16[104,640]{1,0:T(8,128)(2,1)S(1)}, bf16[104,640]{1,0:T(8,128)(2,1)S(1)}, u32[]{:S(2)}, u32[]{:S(2)}) %collective-permute-start.16) | collective-permute-done | bytes 133152 | tf_op jit(solution)/shard_map/ppermute | solution.py:49
  31.8 2.0 %collective-permute-start.17 = (bf16[96,640]{1,0:T(8,128)(2,1)S(1)}, bf16[96,640]{1,0:T(8,128)(2,1)S(1)}, u32[]{:S(2)}, u32[]{:S(2)}) collective-permute-start(bf16[96,640]{1,0:T(8,128)(2,1)S(1)} %collective-permute-done.7.refs_2_), channel_id=1, source_target_pairs={{0,16},{1,17},{2,18},{3,19},{4,20},{5,21},{6,22},{7,23},{8,24},{9,... | collective-permute-start | bytes 368648 | tf_op jit(solution)/shard_map/ppermute | solution.py:49
  33.8 2.9 %collective-permute-done.17.refs_2_ = bf16[96,640]{1,0:T(8,128)(2,1)S(1)} collective-permute-done((bf16[96,640]{1,0:T(8,128)(2,1)S(1)}, bf16[96,640]{1,0:T(8,128)(2,1)S(1)}, u32[]{:S(2)}, u32[]{:S(2)}) %collective-permute-start.17) | collective-permute-done | bytes 122912 | tf_op jit(solution)/shard_map/ppermute | solution.py:49
  36.6 2.0 %collective-permute-start.15 = (bf16[200,640]{1,0:T(8,128)(2,1)S(1)}, bf16[200,640]{1,0:T(8,128)(2,1)S(1)}, u32[]{:S(2)}, u32[]{:S(2)}) collective-permute-start(bf16[200,640]{1,0:T(8,128)(2,1)S(1)} %shard_map.103), channel_id=1, source_target_pairs={{0,16},{1,17},{2,18},{3,19},{4,20},{5,21},{6,22},{7,23},{8,28},{9,... | collective-permute-start | bytes 768008 | tf_op jit(solution)/shard_map/ppermute | solution.py:49
  38.7 1.7 %collective-permute-start.18 = (bf16[200,640]{1,0:T(8,128)(2,1)S(1)}, bf16[200,640]{1,0:T(8,128)(2,1)S(1)}, u32[]{:S(2)}, u32[]{:S(2)}) collective-permute-start(bf16[200,640]{1,0:T(8,128)(2,1)S(1)} %collective-permute-done.8.refs_3_), channel_id=1, source_target_pairs={{0,16},{1,17},{2,18},{3,19},{4,20},{5,21},{6,22},{7,23},{8,24},{9,... | collective-permute-start | bytes 768008 | tf_op jit(solution)/shard_map/ppermute | solution.py:49
  40.4 5.3 %collective-permute-done.15.refs_0_.refs_5_.refs_6_ = bf16[200,640]{1,0:T(8,128)(2,1)S(1)} collective-permute-done((bf16[200,640]{1,0:T(8,128)(2,1)S(1)}, bf16[200,640]{1,0:T(8,128)(2,1)S(1)}, u32[]{:S(2)}, u32[]{:S(2)}) %collective-permute-start.15) | collective-permute-done | bytes 256032 | tf_op jit(solution)/shard_map/ppermute | solution.py:49
  46.4 4.1 %collective-permute-done.18.refs_3_ = bf16[200,640]{1,0:T(8,128)(2,1)S(1)} collective-permute-done((bf16[200,640]{1,0:T(8,128)(2,1)S(1)}, bf16[200,640]{1,0:T(8,128)(2,1)S(1)}, u32[]{:S(2)}, u32[]{:S(2)}) %collective-permute-start.18) | collective-permute-done | bytes 256032 | tf_op jit(solution)/shard_map/ppermute | solution.py:49
  50.5 2.0 %collective-permute-start.20 = (bf16[96,640]{1,0:T(8,128)(2,1)S(1)}, bf16[96,640]{1,0:T(8,128)(2,1)S(1)}, u32[]{:S(2)}, u32[]{:S(2)}) collective-permute-start(bf16[96,640]{1,0:T(8,128)(2,1)S(1)} %collective-permute-done.17.refs_2_), channel_id=1, source_target_pairs={{0,1},{1,0},{2,3},{3,2},{4,5},{5,4},{6,7},{7,6},{8,9},{9,8},{10,11... | collective-permute-start | bytes 368648 | tf_op jit(solution)/shard_map/ppermute | solution.py:49
  52.5 2.1 %shard_map.104 = (bf16[2560,256]{1,0:T(8,128)(2,1)S(1)}, bf16[2560,256]{1,0:T(8,128)(2,1)S(1)}, bf16[256,2560]{1,0:T(8,128)(2,1)S(1)}) custom-call(bf16[2560,256]{1,0:T(8,128)(2,1)} %bitcast.6, bf16[2560,256]{1,0:T(8,128)(2,1)} %bitcast.8, bf16[256,2560]{1,0:T(8,128)(2,1)} %bitcast.10), custom_call_target="tpu_custom_call" | custom-call | tf_op jit(solution)/shard_map/pallas_call | solution.py:175
  57.9 1.6 %collective-permute-done.20.refs_4_ = bf16[96,640]{1,0:T(8,128)(2,1)S(1)} collective-permute-done((bf16[96,640]{1,0:T(8,128)(2,1)S(1)}, bf16[96,640]{1,0:T(8,128)(2,1)S(1)}, u32[]{:S(2)}, u32[]{:S(2)}) %collective-permute-start.20) | collective-permute-done | bytes 122912 | tf_op jit(solution)/shard_map/ppermute | solution.py:49
  59.5 2.6 %shard_map.108 = (bf16[192,640]{1,0:T(8,128)(2,1)S(1)}, bf16[192,640]{1,0:T(8,128)(2,1)S(1)}, bf16[192,640]{1,0:T(8,128)(2,1)S(1)}, bf16[96,640]{1,0:T(8,128)(2,1)S(1)}, bf16[96,640]{1,0:T(8,128)(2,1)S(1)}) custom-call(s32[1]{0:T(128)} %bitcast.where_ref, f32[192,512]{1,0:T(8,128)S(1)} %get-tuple-element.47.refs_0_, ...), custom_call_target="tpu_custom_call" | custom-call | flops 754974720 | bytes 8388608 | tf_op jit(solution)/shard_map/pallas_call | solution.py:260
  63.7 1.7 %collective-permute-start.30 = (bf16[96,640]{1,0:T(8,128)(2,1)S(1)}, bf16[96,640]{1,0:T(8,128)(2,1)S(1)}, u32[]{:S(2)}, u32[]{:S(2)}) collective-permute-start(bf16[96,640]{1,0:T(8,128)(2,1)S(1)} %get-tuple-element.58), channel_id=1, source_target_pairs={{0,1},{1,0},{2,3},{3,2},{4,5},{5,4},{6,7},{7,6},{8,9},{9,8},{10,11... | collective-permute-start | bytes 368648 | tf_op jit(solution)/shard_map/ppermute | solution.py:49
  66.5 2.6 %shard_map.106 = (bf16[192,640]{1,0:T(8,128)(2,1)S(1)}, bf16[192,640]{1,0:T(8,128)(2,1)S(1)}, bf16[192,640]{1,0:T(8,128)(2,1)S(1)}, bf16[96,640]{1,0:T(8,128)(2,1)S(1)}, bf16[96,640]{1,0:T(8,128)(2,1)S(1)}) custom-call(s32[1]{0:T(128)} %bitcast.where_ref, f32[192,512]{1,0:T(8,128)S(1)} %get-tuple-element.42.refs_0_, ...), custom_call_target="tpu_custom_call" | custom-call | flops 754974720 | bytes 8388608 | tf_op jit(solution)/shard_map/pallas_call | solution.py:260
  75.7 1.5 %collective-permute-done.31.refs_2_ = bf16[96,640]{1,0:T(8,128)(2,1)S(1)} collective-permute-done((bf16[96,640]{1,0:T(8,128)(2,1)S(1)}, bf16[96,640]{1,0:T(8,128)(2,1)S(1)}, u32[]{:S(2)}, u32[]{:S(2)}) %collective-permute-start.31) | collective-permute-done | bytes 122912 | tf_op jit(solution)/shard_map/ppermute | solution.py:49
  78.2 3.8 %collective-permute-start.32 = (bf16[96,640]{1,0:T(8,128)(2,1)S(1)}, bf16[96,640]{1,0:T(8,128)(2,1)S(1)}, u32[]{:S(2)}, u32[]{:S(2)}) collective-permute-start(bf16[96,640]{1,0:T(8,128)(2,1)S(1)} %shard_map.115), channel_id=1, source_target_pairs={{0,2},{1,3},{2,0},{3,1},{4,6},{5,7},{6,4},{7,5},{8,14},{9,15},{10,... | collective-permute-start | bytes 368648 | tf_op jit(solution)/shard_map/ppermute | solution.py:49
  82.7 3.5 %collective-permute-start.27 = (bf16[96,640]{1,0:T(8,128)(2,1)S(1)}, bf16[96,640]{1,0:T(8,128)(2,1)S(1)}, u32[]{:S(2)}, u32[]{:S(2)}) collective-permute-start(bf16[96,640]{1,0:T(8,128)(2,1)S(1)} %shard_map.112), channel_id=1, source_target_pairs={{0,2},{1,3},{2,0},{3,1},{4,6},{5,7},{6,4},{7,5},{8,14},{9,15},{10,... | collective-permute-start | bytes 368648 | tf_op jit(solution)/shard_map/ppermute | solution.py:49
  86.2 4.2 %collective-permute-done.32 = bf16[96,640]{1,0:T(8,128)(2,1)S(1)} collective-permute-done((bf16[96,640]{1,0:T(8,128)(2,1)S(1)}, bf16[96,640]{1,0:T(8,128)(2,1)S(1)}, u32[]{:S(2)}, u32[]{:S(2)}) %collective-permute-start.32) | collective-permute-done | bytes 122912 | tf_op jit(solution)/shard_map/ppermute | solution.py:49
  (61 shorter events, 22.5 us)
Async XLA Ops:
  0.0 50.5 %collective-permute-start.9 = (bf16[2560,256]{1,0:T(8,128)(2,1)}, bf16[2560,256]{1,0:T(8,128)(2,1)S(1)}, u32[]{:S(2)}, u32[]{:S(2)}) collective-permute-start(bf16[2560,256]{1,0:T(8,128)(2,1)} %bitcast.5), channel_id=1, source_target_pairs={{0,8},{1,9},{2,10},{3,11},{4,12},{5,13},{6,14},{7,15},{8,0},{9,1},... | collective-permute-start | bytes 3932168 | tf_op jit(solution)/shard_map/ppermute | solution.py:49
  0.5 54.2 %collective-permute-start.10 = (bf16[2560,256]{1,0:T(8,128)(2,1)}, bf16[2560,256]{1,0:T(8,128)(2,1)S(1)}, u32[]{:S(2)}, u32[]{:S(2)}) collective-permute-start(bf16[2560,256]{1,0:T(8,128)(2,1)} %bitcast.7), channel_id=1, source_target_pairs={{0,8},{1,9},{2,10},{3,11},{4,12},{5,13},{6,14},{7,15},{8,0},{9,1},... | collective-permute-start | bytes 3932168 | tf_op jit(solution)/shard_map/ppermute | solution.py:49
  0.5 59.0 %collective-permute-start.13 = (bf16[256,2560]{1,0:T(8,128)(2,1)}, bf16[256,2560]{1,0:T(8,128)(2,1)}, u32[]{:S(2)}, u32[]{:S(2)}) collective-permute-start(bf16[256,2560]{1,0:T(8,128)(2,1)} %bitcast.9), channel_id=1, source_target_pairs={{0,8},{1,9},{2,10},{3,11},{4,12},{5,13},{6,14},{7,15},{8,0},{9,1},... | collective-permute-start | bytes 3932168 | tf_op jit(solution)/shard_map/ppermute | solution.py:49
  1.8 6.5 %collective-permute-start.1 = (bf16[256,128]{1,0:T(8,128)(2,1)S(1)}, bf16[256,128]{1,0:T(8,128)(2,1)S(1)}, u32[]{:S(2)}, u32[]{:S(2)}) collective-permute-start(bf16[256,128]{1,0:T(8,128)(2,1)S(1)} %shard_map.101.refs_0_), channel_id=1, source_target_pairs={{0,16},{1,17},{2,18},{3,19},{4,20},{5,21},{6,22},{7,23},{8,24},{9,... | collective-permute-start | bytes 196616 | tf_op jit(solution)/shard_map/ppermute | solution.py:49
  13.9 12.6 %collective-permute-start.6 = (bf16[104,640]{1,0:T(8,128)(2,1)S(1)}, bf16[104,640]{1,0:T(8,128)(2,1)S(1)}, u32[]{:S(2)}, u32[]{:S(2)}) collective-permute-start(bf16[104,640]{1,0:T(8,128)(2,1)S(1)} %get-tuple-element.37.keep_ref), channel_id=1, source_target_pairs={{0,2},{1,3},{2,0},{3,1},{4,6},{5,7},{6,4},{7,5},{8,14},{9,15},{10,... | collective-permute-start | bytes 399368 | tf_op jit(solution)/shard_map/ppermute | solution.py:49
  16.5 12.7 %collective-permute-start.7 = (bf16[96,640]{1,0:T(8,128)(2,1)S(1)}, bf16[96,640]{1,0:T(8,128)(2,1)S(1)}, u32[]{:S(2)}, u32[]{:S(2)}) collective-permute-start(bf16[96,640]{1,0:T(8,128)(2,1)S(1)} %collective-permute-done.3.got_ref), channel_id=1, source_target_pairs={{0,2},{1,3},{2,0},{3,1},{4,6},{5,7},{6,4},{7,5},{8,14},{9,15},{10,... | collective-permute-start | bytes 368648 | tf_op jit(solution)/shard_map/ppermute | solution.py:49
  29.2 9.5 %collective-permute-start.8 = (bf16[200,640]{1,0:T(8,128)(2,1)S(1)}, bf16[200,640]{1,0:T(8,128)(2,1)S(1)}, u32[]{:S(2)}, u32[]{:S(2)}) collective-permute-start(bf16[200,640]{1,0:T(8,128)(2,1)S(1)} %shard_map.103), channel_id=1, source_target_pairs={{0,1},{1,0},{2,3},{3,2},{4,5},{5,4},{6,7},{7,6},{8,13},{9,12},{10,... | collective-permute-start | bytes 768008 | tf_op jit(solution)/shard_map/ppermute | solution.py:49
  36.6 9.0 %collective-permute-start.15 = (bf16[200,640]{1,0:T(8,128)(2,1)S(1)}, bf16[200,640]{1,0:T(8,128)(2,1)S(1)}, u32[]{:S(2)}, u32[]{:S(2)}) collective-permute-start(bf16[200,640]{1,0:T(8,128)(2,1)S(1)} %shard_map.103), channel_id=1, source_target_pairs={{0,16},{1,17},{2,18},{3,19},{4,20},{5,21},{6,22},{7,23},{8,28},{9,... | collective-permute-start | bytes 768008 | tf_op jit(solution)/shard_map/ppermute | solution.py:49
  38.7 11.8 %collective-permute-start.18 = (bf16[200,640]{1,0:T(8,128)(2,1)S(1)}, bf16[200,640]{1,0:T(8,128)(2,1)S(1)}, u32[]{:S(2)}, u32[]{:S(2)}) collective-permute-start(bf16[200,640]{1,0:T(8,128)(2,1)S(1)} %collective-permute-done.8.refs_3_), channel_id=1, source_target_pairs={{0,16},{1,17},{2,18},{3,19},{4,20},{5,21},{6,22},{7,23},{8,24},{9,... | collective-permute-start | bytes 768008 | tf_op jit(solution)/shard_map/ppermute | solution.py:49
  45.7 18.0 %collective-permute-start.5 = (bf16[200,640]{1,0:T(8,128)(2,1)S(1)}, bf16[200,640]{1,0:T(8,128)(2,1)S(1)}, u32[]{:S(2)}, u32[]{:S(2)}) collective-permute-start(bf16[200,640]{1,0:T(8,128)(2,1)S(1)} %shard_map.103), channel_id=1, source_target_pairs={{0,0},{1,1},{2,2},{3,3},{4,4},{5,5},{6,6},{7,7},{8,12},{9,13},{10,... | collective-permute-start | bytes 768008 | tf_op jit(solution)/shard_map/ppermute | solution.py:49
  50.5 6.4 %collective-permute-start.19 = (bf16[104,640]{1,0:T(8,128)(2,1)S(1)}, bf16[104,640]{1,0:T(8,128)(2,1)S(1)}, u32[]{:S(2)}, u32[]{:S(2)}) collective-permute-start(bf16[104,640]{1,0:T(8,128)(2,1)S(1)} %collective-permute-done.16.refs_1_), channel_id=1, source_target_pairs={{0,1},{1,0},{2,3},{3,2},{4,5},{5,4},{6,7},{7,6},{8,9},{9,8},{10,11... | collective-permute-start | bytes 399368 | tf_op jit(solution)/shard_map/ppermute | solution.py:49
  50.5 9.0 %collective-permute-start.20 = (bf16[96,640]{1,0:T(8,128)(2,1)S(1)}, bf16[96,640]{1,0:T(8,128)(2,1)S(1)}, u32[]{:S(2)}, u32[]{:S(2)}) collective-permute-start(bf16[96,640]{1,0:T(8,128)(2,1)S(1)} %collective-permute-done.17.refs_2_), channel_id=1, source_target_pairs={{0,1},{1,0},{2,3},{3,2},{4,5},{5,4},{6,7},{7,6},{8,9},{9,8},{10,11... | collective-permute-start | bytes 368648 | tf_op jit(solution)/shard_map/ppermute | solution.py:49
  54.7 11.9 %collective-permute-start.11 = (bf16[104,640]{1,0:T(8,128)(2,1)S(1)}, bf16[104,640]{1,0:T(8,128)(2,1)S(1)}, u32[]{:S(2)}, u32[]{:S(2)}) collective-permute-start(bf16[104,640]{1,0:T(8,128)(2,1)S(1)} %collective-permute-done.6.refs_1_), channel_id=1, source_target_pairs={{0,1},{1,0},{2,3},{3,2},{4,5},{5,4},{6,7},{7,6},{8,9},{9,8},{10,11... | collective-permute-start | bytes 399368 | tf_op jit(solution)/shard_map/ppermute | solution.py:49
  56.9 9.6 %collective-permute-start.12 = (bf16[96,640]{1,0:T(8,128)(2,1)S(1)}, bf16[96,640]{1,0:T(8,128)(2,1)S(1)}, u32[]{:S(2)}, u32[]{:S(2)}) collective-permute-start(bf16[96,640]{1,0:T(8,128)(2,1)S(1)} %collective-permute-done.7.refs_2_), channel_id=1, source_target_pairs={{0,1},{1,0},{2,3},{3,2},{4,5},{5,4},{6,7},{7,6},{8,9},{9,8},{10,11... | collective-permute-start | bytes 368648 | tf_op jit(solution)/shard_map/ppermute | solution.py:49
  62.2 9.7 %collective-permute-start.22 = (bf16[192,640]{1,0:T(8,128)(2,1)S(1)}, bf16[192,640]{1,0:T(8,128)(2,1)S(1)}, u32[]{:S(2)}, u32[]{:S(2)}) collective-permute-start(bf16[192,640]{1,0:T(8,128)(2,1)S(1)} %get-tuple-element.52), channel_id=1, source_target_pairs={{0,16},{1,17},{2,18},{3,19},{4,20},{5,21},{6,22},{7,23},{8,24},{9,... | collective-permute-start | bytes 737288 | tf_op jit(solution)/shard_map/ppermute | solution.py:49
  63.4 9.6 %collective-permute-start.25 = (bf16[96,640]{1,0:T(8,128)(2,1)S(1)}, bf16[96,640]{1,0:T(8,128)(2,1)S(1)}, u32[]{:S(2)}, u32[]{:S(2)}) collective-permute-start(bf16[96,640]{1,0:T(8,128)(2,1)S(1)} %get-tuple-element.56), channel_id=1, source_target_pairs={{0,1},{1,0},{2,3},{3,2},{4,5},{5,4},{6,7},{7,6},{8,9},{9,8},{10,11... | collective-permute-start | bytes 368648 | tf_op jit(solution)/shard_map/ppermute | solution.py:49
  63.7 7.2 %collective-permute-start.30 = (bf16[96,640]{1,0:T(8,128)(2,1)S(1)}, bf16[96,640]{1,0:T(8,128)(2,1)S(1)}, u32[]{:S(2)}, u32[]{:S(2)}) collective-permute-start(bf16[96,640]{1,0:T(8,128)(2,1)S(1)} %get-tuple-element.58), channel_id=1, source_target_pairs={{0,1},{1,0},{2,3},{3,2},{4,5},{5,4},{6,7},{7,6},{8,9},{9,8},{10,11... | collective-permute-start | bytes 368648 | tf_op jit(solution)/shard_map/ppermute | solution.py:49
  69.6 20.8 %collective-permute-start.14 = (bf16[192,640]{1,0:T(8,128)(2,1)S(1)}, bf16[192,640]{1,0:T(8,128)(2,1)S(1)}, u32[]{:S(2)}, u32[]{:S(2)}) collective-permute-start(bf16[192,640]{1,0:T(8,128)(2,1)S(1)} %get-tuple-element.46), channel_id=1, source_target_pairs={{0,0},{1,1},{2,2},{3,3},{4,4},{5,5},{6,6},{7,7},{8,12},{9,13},{10,... | collective-permute-start | bytes 737288 | tf_op jit(solution)/shard_map/ppermute | solution.py:49
  70.9 6.3 %collective-permute-start.31 = (bf16[96,640]{1,0:T(8,128)(2,1)S(1)}, bf16[96,640]{1,0:T(8,128)(2,1)S(1)}, u32[]{:S(2)}, u32[]{:S(2)}) collective-permute-start(bf16[96,640]{1,0:T(8,128)(2,1)S(1)} %shard_map.114), channel_id=1, source_target_pairs={{0,16},{1,17},{2,18},{3,19},{4,20},{5,21},{6,22},{7,23},{8,24},{9,... | collective-permute-start | bytes 368648 | tf_op jit(solution)/shard_map/ppermute | solution.py:49
  71.9 6.4 %collective-permute-start.24 = (bf16[96,640]{1,0:T(8,128)(2,1)S(1)}, bf16[96,640]{1,0:T(8,128)(2,1)S(1)}, u32[]{:S(2)}, u32[]{:S(2)}) collective-permute-start(bf16[96,640]{1,0:T(8,128)(2,1)S(1)} %get-tuple-element.54), channel_id=1, source_target_pairs={{0,1},{1,0},{2,3},{3,2},{4,5},{5,4},{6,7},{7,6},{8,9},{9,8},{10,11... | collective-permute-start | bytes 368648 | tf_op jit(solution)/shard_map/ppermute | solution.py:49
  73.0 17.4 %collective-permute-start.21 = (bf16[192,640]{1,0:T(8,128)(2,1)S(1)}, bf16[192,640]{1,0:T(8,128)(2,1)S(1)}, u32[]{:S(2)}, u32[]{:S(2)}) collective-permute-start(bf16[192,640]{1,0:T(8,128)(2,1)S(1)} %get-tuple-element.50), channel_id=1, source_target_pairs={{0,16},{1,17},{2,18},{3,19},{4,20},{5,21},{6,22},{7,23},{8,28},{9,... | collective-permute-start | bytes 737288 | tf_op jit(solution)/shard_map/ppermute | solution.py:49
  74.7 15.7 %collective-permute-start.23 = (bf16[192,640]{1,0:T(8,128)(2,1)S(1)}, bf16[192,640]{1,0:T(8,128)(2,1)S(1)}, u32[]{:S(2)}, u32[]{:S(2)}) collective-permute-start(bf16[192,640]{1,0:T(8,128)(2,1)S(1)} %shard_map.109), channel_id=1, source_target_pairs={{0,1},{1,0},{2,3},{3,2},{4,5},{5,4},{6,7},{7,6},{8,13},{9,12},{10,... | collective-permute-start | bytes 737288 | tf_op jit(solution)/shard_map/ppermute | solution.py:49
  78.2 12.1 %collective-permute-start.32 = (bf16[96,640]{1,0:T(8,128)(2,1)S(1)}, bf16[96,640]{1,0:T(8,128)(2,1)S(1)}, u32[]{:S(2)}, u32[]{:S(2)}) collective-permute-start(bf16[96,640]{1,0:T(8,128)(2,1)S(1)} %shard_map.115), channel_id=1, source_target_pairs={{0,2},{1,3},{2,0},{3,1},{4,6},{5,7},{6,4},{7,5},{8,14},{9,15},{10,... | collective-permute-start | bytes 368648 | tf_op jit(solution)/shard_map/ppermute | solution.py:49
  82.7 9.5 %collective-permute-start.27 = (bf16[96,640]{1,0:T(8,128)(2,1)S(1)}, bf16[96,640]{1,0:T(8,128)(2,1)S(1)}, u32[]{:S(2)}, u32[]{:S(2)}) collective-permute-start(bf16[96,640]{1,0:T(8,128)(2,1)S(1)} %shard_map.112), channel_id=1, source_target_pairs={{0,2},{1,3},{2,0},{3,1},{4,6},{5,7},{6,4},{7,5},{8,14},{9,15},{10,... | collective-permute-start | bytes 368648 | tf_op jit(solution)/shard_map/ppermute | solution.py:49
  (10 other events, 36.0 us)
